TPU v7x, 32 devices: a whole 2x2x4 slice. The times are simulated.
32 devices in a mesh: gx: 8 (over y, x, core), gy: 4 (over z).
Axes of the slice: x: 2, y: 2, z: 4, core: 2. Of those that a mesh axis runs over, the one named last changes fastest.
Arguments:
- latent: bfloat16 [13824, 128], P(('gx', 'gy')), may hold values from -6 to 6
- offset: bfloat16 [2, 13824], P(None, ('gx', 'gy')), may hold values from 0 to 1
- owner: int32 [13824], P(('gx', 'gy')), may hold values from 0 to 31, as said below
- slot: int32 [13824], P(('gx', 'gy')), may hold values from -1 to 511, as said below
- cotangent: bfloat16 [64, 32, 8, 128], P('gx', 'gy'), may hold values from -6 to 6
- edge_in: bfloat16 [2, 128, 256], replicated, may hold values from -0.5 to 0.5
- edge_geo: bfloat16 [2, 3, 128], replicated, may hold values from -3.5 to 3.5
- edge_mid: bfloat16 [2, 128, 128], replicated, may hold values from -0.5 to 0.5
- edge_out: bfloat16 [2, 128, 128], replicated, may hold values from -0.25 to 0.25
- node_in: bfloat16 [2, 256, 128], replicated, may hold values from -0.375 to 0.375
- node_out: bfloat16 [2, 128, 128], replicated, may hold values from -0.5 to 0.5
- biases: bfloat16 [2, 5, 128], replicated, may hold values from -3 to 3
- ln_gain: bfloat16 [2, 128], replicated, may hold values from 0.5 to 1.5
Outputs:
- latent_out: bfloat16 [64, 32, 8, 128], P('gx', 'gy')
- latent_grad: float32 [64, 32, 8, 128], P('gx', 'gy')
- grad_edge_in: float32 [2, 128, 256], replicated
- grad_edge_geo: float32 [2, 3, 128], replicated
- grad_edge_mid: float32 [2, 128, 128], replicated
- grad_edge_out: float32 [2, 128, 128], replicated
- grad_node_in: float32 [2, 256, 128], replicated
- grad_node_out: float32 [2, 128, 128], replicated
- grad_biases: float32 [2, 5, 128], replicated
- grad_ln_gain: float32 [2, 128], replicated
Inputs may be any that keep to these rules, and one draw needn't show every extreme that they name: `owner`: the 432 rows of each device name each of the nine devices at offsets -1, 0, +1 along gx and along gy (wrapping around, the device itself included) exactly 48 times. Cell (cx, cy) of a device holds slots (cx * 8 + cy) * 8 to (cx * 8 + cy) * 8 + 7. No slot of a device is named by two rows. In every draw some cell of every device receives 8 particles, and every device has 48 rows with particles for one of its neighbours.
All inputs are finite; a program needn't handle non-finite values.
Results may differ from a plain program's by a relative error of at most 0.019.
Values may be sent and summed in bfloat16 or wider, within the bound.
No kernel may reach another device: no remote copies, remote signals or barrier semaphores. Data moves between devices by JAX's collectives and lax.ppermute only.
A program may use at most 64 MiB of HBM per device.

v0:
```python
import functools

import jax
import jax.numpy as jnp
from jax import lax
from jax.experimental import pallas as pl
from jax.experimental.pallas import tpu as pltpu
from jax.sharding import PartitionSpec as P

STEPS = 2
LN_EPS = 1e-05
F32 = jnp.float32
BF = jnp.bfloat16
L = 128
CAP = 8
NEAR = 9 * CAP
EDGES = CAP * NEAR
GROWS = 1024


def dot(a, b):
    return jnp.dot(a, b, preferred_element_type=F32)


def dot_tn(a, b):
    return lax.dot_general(a, b, (((0,), (0,)), ((), ())), preferred_element_type=F32)


def dot_nt(a, b):
    return lax.dot_general(a, b, (((1,), (1,)), ((), ())), preferred_element_type=F32)


def iota(shape, dim):
    return lax.broadcasted_iota(jnp.int32, shape, dim)


def mask(cond):
    return jnp.where(cond, 1.0, 0.0).astype(F32)


def slope_of(half, tanh_half):
    sig = 0.5 + 0.5 * tanh_half
    act = half + half * tanh_half
    return sig + act * (1.0 - sig)


def sort_kernel(latent_ref, bucket_ref, meta_ref, out_ref):
    rows = latent_ref.shape[0]
    send = rows // 9
    bucket = bucket_ref[...]
    hot = mask(iota((16, rows), 0) == bucket)
    upper = mask(iota((rows, rows), 0) <= iota((rows, rows), 1)).astype(BF)
    count = dot(hot.astype(BF), upper)
    rank = jnp.sum(hot * (count - 1.0), axis=0, keepdims=True)
    target = bucket.astype(F32) * float(send) + rank
    perm = mask(iota((rows, rows), 0).astype(F32) == target).astype(BF)
    out_ref[:, :L] = dot(perm, latent_ref[...]).astype(BF)
    meta = jnp.concatenate([meta_ref[...], jnp.zeros((L - 8, rows), F32)], axis=0).astype(BF)
    out_ref[:, L:] = dot_nt(perm, meta).astype(BF)


def place_kernel(rows_ref, edge_in_ref, latent_ref, own_ref, pay_ref):
    rows = rows_ref.shape[0]
    slots = latent_ref.shape[0]
    pick_lane = iota((8, L), 1)
    pick = jnp.where(pick_lane == 3, 16.0, jnp.where(pick_lane == 4, 1.0, 0.0)).astype(BF)
    mark = dot_nt(pick, rows_ref[:, L:])[0:1]
    hot = mask((iota((slots, rows), 0) + 1).astype(F32) == mark).astype(BF)
    placed = dot(hot, rows_ref[...]).astype(BF)
    latent = placed[:, :L]
    latent_ref[...] = latent
    both = dot(latent, edge_in_ref[...])
    own_ref[...] = both[:, :L]
    pay_ref[:, :L] = both[:, L:].astype(BF)
    pay_ref[:, L:] = placed[:, L:]


def fill_geometry(geo, width, lhs_ref, weight_ref, weight_t_ref, radius_t_ref, hot_t_ref):
    halo_rows = geo.shape[0]
    rows = dot_nt(mask(iota((8, L), 0) == iota((8, L), 1)).astype(BF), geo)
    cell = iota((halo_rows, L), 1) * CAP
    row = iota((halo_rows, L), 0)
    cell_hot = mask((row >= cell) & (row < cell + CAP)).astype(BF)
    slot_hot = mask((iota((8, halo_rows), 1) & (CAP - 1)) == iota((8, halo_rows), 0))
    px, py, occ = (dot((slot_hot * rows[k : k + 1]).astype(BF), cell_hot) for k in range(3))
    near = ([], [], [])
    for a in (-1, 0, 1):
        for b in (-1, 0, 1):
            shift = (-(width * a + b)) % L
            for piece, value, base in zip(near, (px, py, occ), (a, b, 0)):
                moved = value if shift == 0 else pltpu.roll(value, shift, 1)
                piece.append(moved + float(base))
    near_x, near_y, near_occ = (jnp.concatenate(piece, axis=0) for piece in near)
    radius, weight, hots = [], [], []
    lane = iota((NEAR, L), 1)
    sub = iota((NEAR, L), 0)
    for i in range(CAP):
        dx = near_x - px[i : i + 1]
        dy = near_y - py[i : i + 1]
        r2 = dx * dx + dy * dy
        reach = jnp.maximum(1.0 - r2, 0.0)
        w = occ[i : i + 1] * near_occ * reach * reach
        radius.append(r2)
        weight.append(jnp.where(sub == 4 * CAP + i, 0.0, w))
        hots.append(mask((sub == lane) | (lane == NEAR + i) | (lane == NEAR + CAP + i)))
    radius = jnp.concatenate(radius, axis=0)
    weight = jnp.concatenate(weight, axis=0)
    hots = jnp.concatenate(hots, axis=0)
    lhs_ref[:, :L] = hots.astype(BF)
    lhs_ref[:, L:] = radius.astype(BF)
    weight_ref[...] = weight.astype(BF)
    weight_t_ref[...] = weight.T
    radius_t_ref[...] = radius.T
    hot_t_ref[...] = hots.T[:80].astype(BF)


def column(value, k):
    return value[:, k : k + 1].astype(F32)


def fill_pre(far, geo_halo, own, geo_own, edge_geo, far_ref, near_ref):
    g0 = 0.5 * edge_geo[0:1].astype(F32)
    g1 = 0.5 * edge_geo[1:2].astype(F32)
    far_ref[...] = 0.5 * far.astype(F32) + column(geo_halo, 0) * g0 + column(geo_halo, 1) * g1
    near_ref[...] = 0.5 * own - column(geo_own, 0) * g0 - column(geo_own, 1) * g1


def shift_rows(edge_geo):
    g0 = 0.5 * edge_geo[0:1].astype(F32)
    g1 = 0.5 * edge_geo[1:2].astype(F32)
    side = iota((3 * CAP, L), 0) // CAP - 1
    return [float(a) * g0 + side.astype(F32) * g1 for a in (-1, 0, 1)]


def twice(row):
    return jnp.concatenate([row, row], axis=1)


def block_diag(w):
    zero = jnp.zeros_like(w)
    return jnp.concatenate(
        [jnp.concatenate([w, zero], axis=1), jnp.concatenate([zero, w], axis=1)], axis=0
    )


def pair_place(pair, cells_y):
    half = cells_y // 2
    x = pair // half
    y = (pair - x * half) * 2
    return x, y


def pair_rhs(pair, width, far_ref, near_ref, shifts, g2):
    x, y = pair_place(pair, width - 2)
    tops = []
    for k in range(2):
        pieces = []
        for a in range(3):
            start = pl.multiple_of(((x + a) * width + y + k) * CAP, CAP)
            pieces.append(far_ref[pl.ds(start, 3 * CAP), :] + shifts[a])
        mine = near_ref[pl.ds(pl.multiple_of((pair * 2 + k) * CAP, CAP), CAP), :]
        pieces.append(mine)
        pieces.append(mine - mine.astype(BF).astype(F32))
        pieces.append(jnp.zeros((L - NEAR - 2 * CAP, L), F32))
        tops.append(jnp.concatenate(pieces, axis=0))
    top = jnp.concatenate(tops, axis=1).astype(BF)
    hot = pair_hot(pair, width)
    return jnp.concatenate([top, jnp.where(hot, g2, 0.0).astype(BF)], axis=0)


def pair_hot(pair, width):
    x, y = pair_place(pair, width - 2)
    first = (x + 1) * width + y + 1
    lane = iota((L, 2 * L), 1)
    return iota((L, 2 * L), 0) == first + jnp.where(lane >= L, 1, 0)


def pair_rows(pair, width, ref):
    x, y = pair_place(pair, width - 2)
    first = (x + 1) * width + y + 1
    return ref[pl.ds(first, 1), :], ref[pl.ds(first + 1, 1), :]


def edges_forward(width, lhs_ref, weight_t_ref, far_ref, near_ref, shifts, g2, mid2_ref, bias2, sums_ref, wsum_ref):
    pairs = sums_ref.shape[0] // (2 * CAP)
    col = iota((CAP, EDGES), 1)
    start = iota((CAP, EDGES), 0) * NEAR
    own = mask((col >= start) & (col < start + NEAR))

    def body(pair, carry):
        rhs = pair_rhs(pair, width, far_ref, near_ref, shifts, g2)
        pre_one = dot(lhs_ref[...], rhs)
        hidden = (pre_one + pre_one * jnp.tanh(pre_one)).astype(BF)
        pre_two = dot(hidden, mid2_ref[...]) + bias2
        act = (pre_two + pre_two * jnp.tanh(pre_two)).astype(BF)
        row_a, row_b = pair_rows(pair, width, weight_t_ref)
        spread = jnp.concatenate([own * row_a, own * row_b], axis=0)
        sums = dot(spread.astype(BF), act)
        at = pl.ds(pl.multiple_of(pair * 2 * CAP, 2 * CAP), 2 * CAP)
        sums_ref[at, :] = jnp.concatenate([sums[:CAP, :L], sums[CAP:, L:]], axis=0)
        wsum_ref[at, :] = jnp.broadcast_to(jnp.sum(spread, axis=1, keepdims=True), (2 * CAP, L))
        return carry

    lax.fori_loop(0, pairs, body, 0)


def edges_backward(
    width, lhs_ref, weight_ref, radius_t_ref, hot_t_ref, far_ref, near_ref, shifts, g2, mid2_ref, mid2_t_ref, bias2,
    d_sums_ref, d_own_ref, d_far_ref, mid_ref, rows_ref, bias_ref,
):
    pairs = d_own_ref.shape[0] // (2 * CAP)
    d_far_ref[...] = jnp.zeros_like(d_far_ref)
    mid_ref[...] = jnp.zeros_like(mid_ref)
    rows_ref[...] = jnp.zeros_like(rows_ref)
    bias_ref[...] = jnp.zeros_like(bias_ref)

    def body(pair, carry):
        x, y = pair_place(pair, width - 2)
        rhs = pair_rhs(pair, width, far_ref, near_ref, shifts, g2)
        pre_one = dot(lhs_ref[...], rhs)
        tanh_one = jnp.tanh(pre_one)
        hidden = (pre_one + pre_one * tanh_one).astype(BF)
        pre_two = dot(hidden, mid2_ref[...]) + bias2
        pick = mask(pair_hot(pair, width)).astype(BF)
        weight = dot(weight_ref[...], pick)
        base = pl.multiple_of(pair * 2 * CAP, 2 * CAP)
        d_sums = d_sums_ref[pl.ds(base, 2 * CAP), :]
        d_sums = jnp.concatenate([d_sums[:CAP], d_sums[CAP:]], axis=1)
        d_sums = jnp.broadcast_to(d_sums[:, None, :], (CAP, NEAR, 2 * L)).reshape(EDGES, 2 * L)
        d_two = weight * d_sums * slope_of(pre_two, jnp.tanh(pre_two))
        bias_ref[...] += jnp.sum(d_two.reshape(EDGES // 8, 8, 2 * L), axis=0)
        d_two = d_two.astype(BF)
        mid_ref[...] += dot_tn(hidden, d_two)
        d_one = (dot(d_two, mid2_t_ref[...]) * slope_of(pre_one, tanh_one)).astype(BF)
        rad_a, rad_b = pair_rows(pair, width, radius_t_ref)
        tail = jnp.concatenate([rad_a, rad_b, jnp.zeros((14, EDGES), F32)], axis=0).astype(BF)
        back = dot(jnp.concatenate([hot_t_ref[...], tail], axis=0), d_one)
        rows_ref[...] += back
        own_rows = back[NEAR : NEAR + CAP]
        d_own_ref[pl.ds(base, 2 * CAP), :] = jnp.concatenate([own_rows[:, :L], own_rows[:, L:]], axis=0)
        for a in range(3):
            piece = back[3 * CAP * a : 3 * CAP * (a + 1)]
            zero = jnp.zeros((CAP, L), F32)
            both = jnp.concatenate([piece[:, :L], zero], axis=0) + jnp.concatenate([zero, piece[:, L:]], axis=0)
            at = pl.ds(pl.multiple_of(((x + a) * width + y) * CAP, CAP), 4 * CAP)
            d_far_ref[at, :] += both
        return carry

    lax.fori_loop(0, pairs, body, 0)


def geo_grads(rows, d_far, geo_halo, d_own, geo_own):
    def total(value):
        return jnp.sum(value, axis=0, keepdims=True)

    rows = jnp.concatenate([rows[: NEAR, :L] + rows[: NEAR, L:], rows[80:82, :L], rows[80:82, L:]], axis=0)
    block = [total(rows[CAP * k : CAP * (k + 1)]) for k in range(9)]
    grad_x = sum(float(k // 3 - 1) * block[k] for k in range(9) if k // 3 != 1)
    grad_y = sum(float(k % 3 - 1) * block[k] for k in range(9) if k % 3 != 1)
    grad_x = grad_x + total(column(geo_halo, 0) * d_far) - total(column(geo_own, 0) * d_own)
    grad_y = grad_y + total(column(geo_halo, 1) * d_far) - total(column(geo_own, 1) * d_own)
    grad_r = rows[NEAR : NEAR + 1] + rows[NEAR + 3 : NEAR + 4]
    return grad_x, grad_y, grad_r


def node_forward(latent, occ, sums, wsum, w_out, w_first, w_second, biases, gain):
    bias = biases.astype(F32)
    sums_low = sums.astype(BF)
    message_low = (dot(sums_low, w_out) + wsum * bias[1:2]).astype(BF)
    first_pre = dot(latent, w_first[:L]) + dot(message_low, w_first[L:]) + bias[2:3]
    half = 0.5 * first_pre
    first_low = (half + half * jnp.tanh(half)).astype(BF)
    second = dot(first_low, w_second) + bias[3:4]
    centred = second - jnp.mean(second, axis=1, keepdims=True)
    inv_root = lax.rsqrt(jnp.mean(centred * centred, axis=1, keepdims=True) + LN_EPS)
    normed = centred * inv_root
    update = normed * gain.astype(F32) + bias[4:5]
    new = (latent.astype(F32) + occ * update).astype(BF)
    return new, (sums_low, message_low, half, first_low, normed, inv_root)


def node_backward(d_new, latent, occ, wsum, saved, w_out, w_first, w_second, gain):
    sums_low, message_low, half, first_low, normed, inv_root = saved

    def total(value):
        return jnp.sum(value, axis=0, keepdims=True)

    d_update = occ * d_new
    grad_gain = total(d_update * normed)
    grad_shift = total(d_update)
    d_normed = d_update * gain.astype(F32)
    d_second = inv_root * (
        d_normed
        - jnp.mean(d_normed, axis=1, keepdims=True)
        - normed * jnp.mean(d_normed * normed, axis=1, keepdims=True)
    )
    d_second_low = d_second.astype(BF)
    grad_second = dot_tn(first_low, d_second_low)
    d_first = dot_nt(d_second_low, w_second) * slope_of(half, jnp.tanh(half))
    d_first_low = d_first.astype(BF)
    grad_first = [dot_tn(latent, d_first_low), dot_tn(message_low, d_first_low)]
    d_latent = dot_nt(d_first_low, w_first[:L])
    d_message = dot_nt(d_first_low, w_first[L:])
    d_message_low = d_message.astype(BF)
    grad_out = dot_tn(sums_low, d_message_low)
    d_sums = dot_nt(d_message_low, w_out)
    small = [total(wsum * d_message), total(d_first), total(d_second), grad_shift, grad_gain]
    return d_sums, d_latent, grad_out, grad_first, grad_second, small


def store_node_grads(grads_ref, small_ref, grad_out, grad_first, grad_second, small):
    base = L
    for block in (grad_out, grad_first[0], grad_first[1], grad_second):
        grads_ref[base : base + L, :] = block
        base += L
    small_ref[...] = jnp.concatenate(small + [jnp.zeros((3, L), F32)], axis=0)


def store_edge_grads(grads_ref, small_ref, mid, bias, geo):
    grads_ref[:L, :] = mid[:L, :L] + mid[L:, L:]
    bias = jnp.sum(bias, axis=0, keepdims=True)
    rows = [bias[:, :L] + bias[:, L:], small_ref[:5, :]] + list(geo)
    grads_ref[5 * L :, :] = jnp.concatenate(rows + [jnp.zeros((L - 9, L), F32)], axis=0)


def edge_constants(edge_geo_ref, mid_ref, biases_ref, mid2_ref, mid2_t_ref=None):
    edge_geo = edge_geo_ref[...]
    mid = mid_ref[...].astype(F32)
    mid2 = block_diag(0.5 * mid).astype(BF)
    bias2 = twice(0.5 * biases_ref[0:1, :].astype(F32))
    g2 = twice(0.5 * edge_geo[2:3].astype(F32))
    mid2_ref[...] = mid2
    if mid2_t_ref is not None:
        mid2_t_ref[...] = block_diag(mid.T).astype(BF)
    return shift_rows(edge_geo), g2, bias2


def first_kernel(
    width, halo_ref, pay_ref, own_ref, latent_ref, edge_geo_ref, mid_w_ref, out_w_ref, first_w_ref, second_w_ref,
    biases_ref, gain_ref, next_in_ref,
    lhs_ref, weight_ref, weight_t_ref, radius_t_ref, hot_t_ref, new_ref, next_own_ref, next_far_ref,
    wsum_ref, sums_low_ref, message_ref, half_ref, first_low_ref, normed_ref, inv_ref,
    far_ref, near_ref, sums_ref, mid2_ref,
):
    fill_geometry(halo_ref[:, L:], width, lhs_ref, weight_ref, weight_t_ref, radius_t_ref, hot_t_ref)
    fill_pre(halo_ref[:, :L], halo_ref[:, L:], own_ref[...], pay_ref[:, L:], edge_geo_ref[...], far_ref, near_ref)
    shifts, g2, bias2 = edge_constants(edge_geo_ref, mid_w_ref, biases_ref, mid2_ref)
    edges_forward(width, lhs_ref, weight_t_ref, far_ref, near_ref, shifts, g2, mid2_ref, bias2, sums_ref, wsum_ref)
    occ = column(pay_ref[:, L:], 2)
    new, saved = node_forward(
        latent_ref[...], occ, sums_ref[...], wsum_ref[...], out_w_ref[...], first_w_ref[...], second_w_ref[...],
        biases_ref[...], gain_ref[...],
    )
    for ref, value in zip((sums_low_ref, message_ref, half_ref, first_low_ref, normed_ref), saved):
        ref[...] = value
    inv_ref[...] = jnp.broadcast_to(saved[5], inv_ref.shape)
    new_ref[...] = new
    both = dot(new, next_in_ref[...])
    next_own_ref[...] = both[:, :L]
    next_far_ref[...] = both[:, L:].astype(BF)


def middle_kernel(
    width, far_in_ref, halo_ref, pay_ref, own_ref, latent_ref, cot_ref, lhs_ref, weight_ref, weight_t_ref,
    radius_t_ref, hot_t_ref, edge_geo_ref, mid_w_ref, out_w_ref, first_w_ref, second_w_ref, biases_ref, gain_ref,
    new_ref, d_own_ref, d_far_ref, grad_ref, grads_ref,
    far_ref, near_ref, sums_ref, wsum_ref, mid_ref, rows_ref, bias_ref, mid2_ref, mid2_t_ref, small_ref,
):
    fill_pre(far_in_ref[...], halo_ref[:, L:], own_ref[...], pay_ref[:, L:], edge_geo_ref[...], far_ref, near_ref)
    shifts, g2, bias2 = edge_constants(edge_geo_ref, mid_w_ref, biases_ref, mid2_ref, mid2_t_ref)
    edges_forward(width, lhs_ref, weight_t_ref, far_ref, near_ref, shifts, g2, mid2_ref, bias2, sums_ref, wsum_ref)
    occ = column(pay_ref[:, L:], 2)
    new, saved = node_forward(
        latent_ref[...], occ, sums_ref[...], wsum_ref[...], out_w_ref[...], first_w_ref[...], second_w_ref[...],
        biases_ref[...], gain_ref[...],
    )
    new_ref[...] = new
    d_new = cot_ref[...].astype(F32)
    d_sums, d_latent, grad_out, grad_first, grad_second, small = node_backward(
        d_new, latent_ref[...], occ, wsum_ref[...], saved, out_w_ref[...], first_w_ref[...], second_w_ref[...],
        gain_ref[...],
    )
    sums_ref[...] = d_sums
    grad_ref[...] = d_new + d_latent
    store_node_grads(grads_ref, small_ref, grad_out, grad_first, grad_second, small)
    edges_backward(
        width, lhs_ref, weight_ref, radius_t_ref, hot_t_ref, far_ref, near_ref, shifts, g2, mid2_ref, mid2_t_ref, bias2,
        sums_ref, d_own_ref, d_far_ref, mid_ref, rows_ref, bias_ref,
    )
    geo = geo_grads(rows_ref[...], d_far_ref[...], halo_ref[:, L:], d_own_ref[...], pay_ref[:, L:])
    store_edge_grads(grads_ref, small_ref, mid_ref[...], bias_ref[...], geo)


def back_kernel(
    width, next_d_own_ref, next_d_far_ref, next_grad_ref, next_latent_ref, next_in_ref, halo_ref, pay_ref, own_ref,
    latent_ref, lhs_ref, weight_ref, radius_t_ref, hot_t_ref, wsum_ref, sums_low_ref, message_ref, half_ref,
    first_low_ref, normed_ref, inv_ref,
    edge_geo_ref, mid_w_ref, out_w_ref, first_w_ref, second_w_ref, biases_ref, gain_ref,
    d_own_ref, d_far_ref, grad_ref, grads_ref, grad_in_ref,
    far_ref, near_ref, sums_ref, mid_ref, rows_ref, bias_ref, mid2_ref, mid2_t_ref, small_ref,
):
    d_both = jnp.concatenate([next_d_own_ref[...], next_d_far_ref[...]], axis=1).astype(BF)
    grad_in_ref[...] = dot_tn(next_latent_ref[...], d_both)
    d_new = next_grad_ref[...] + dot_nt(d_both, next_in_ref[...])
    fill_pre(halo_ref[:, :L], halo_ref[:, L:], own_ref[...], pay_ref[:, L:], edge_geo_ref[...], far_ref, near_ref)
    shifts, g2, bias2 = edge_constants(edge_geo_ref, mid_w_ref, biases_ref, mid2_ref, mid2_t_ref)
    occ = column(pay_ref[:, L:], 2)
    saved = (
        sums_low_ref[...], message_ref[...], half_ref[...], first_low_ref[...], normed_ref[...], inv_ref[...],
    )
    d_sums, d_latent, grad_out, grad_first, grad_second, small = node_backward(
        d_new, latent_ref[...], occ, wsum_ref[...], saved, out_w_ref[...], first_w_ref[...], second_w_ref[...],
        gain_ref[...],
    )
    sums_ref[...] = d_sums
    grad_ref[...] = d_new + d_latent
    store_node_grads(grads_ref, small_ref, grad_out, grad_first, grad_second, small)
    edges_backward(
        width, lhs_ref, weight_ref, radius_t_ref, hot_t_ref, far_ref, near_ref, shifts, g2, mid2_ref, mid2_t_ref, bias2,
        sums_ref, d_own_ref, d_far_ref, mid_ref, rows_ref, bias_ref,
    )
    geo = geo_grads(rows_ref[...], d_far_ref[...], halo_ref[:, L:], d_own_ref[...], pay_ref[:, L:])
    store_edge_grads(grads_ref, small_ref, mid_ref[...], bias_ref[...], geo)


def last_kernel(d_own_ref, d_far_ref, grad_ref, latent_ref, edge_in_ref, pay_ref, out_ref, grad_in_ref):
    d_both = jnp.concatenate([d_own_ref[...], d_far_ref[...]], axis=1).astype(BF)
    grad_in_ref[...] = dot_tn(latent_ref[...], d_both)
    occ = column(pay_ref[:, L:], 2)
    out_ref[...] = occ * (grad_ref[...] + dot_nt(d_both, edge_in_ref[...]))


def call(kernel, outs, scratch, *args):
    return pl.pallas_call(
        kernel,
        out_shape=[jax.ShapeDtypeStruct(shape, dtype) for shape, dtype in outs],
        in_specs=[pl.BlockSpec(memory_space=pltpu.VMEM)] * len(args),
        out_specs=[pl.BlockSpec(memory_space=pltpu.VMEM)] * len(outs),
        scratch_shapes=[pltpu.VMEM(shape, dtype) for shape, dtype in scratch],
        compiler_params=pltpu.CompilerParams(vmem_limit_bytes=48 * 1024 * 1024),
    )(*args)


def from_behind(value, axis, steps):
    count = lax.axis_size(axis)
    return lax.ppermute(value, axis, [(source, (source + steps) % count) for source in range(count)])


def with_halo(block):
    for axis, dim in (("gx", 0), ("gy", 1)):
        size = block.shape[dim]
        low = from_behind(lax.slice_in_dim(block, size - 1, size, axis=dim), axis, 1)
        high = from_behind(lax.slice_in_dim(block, 0, 1, axis=dim), axis, -1)
        block = jnp.concatenate([low, block, high], axis=dim)
    return block


def fold_halo(block):
    for axis, dim in (("gx", 0), ("gy", 1)):
        size = block.shape[dim]
        high = from_behind(lax.slice_in_dim(block, 0, 1, axis=dim).astype(BF), axis, -1).astype(F32)
        low = from_behind(lax.slice_in_dim(block, size - 1, size, axis=dim).astype(BF), axis, 1).astype(F32)
        inner = lax.slice_in_dim(block, 1, size - 1, axis=dim)
        first = lax.slice_in_dim(inner, 0, 1, axis=dim) + low
        last = lax.slice_in_dim(inner, size - 3, size - 2, axis=dim) + high
        block = jnp.concatenate([first, lax.slice_in_dim(inner, 1, size - 3, axis=dim), last], axis=dim)
    return block


def total_over_devices(rows):
    axes = ("gx", "gy")
    count = lax.axis_size("gx") * lax.axis_size("gy")
    parts = lax.all_to_all(rows.astype(BF).reshape(count, -1, L), axes, 0, 0)
    mine = jnp.sum(parts.astype(F32), axis=0).astype(BF)
    spread = jnp.broadcast_to(mine[None], (count,) + mine.shape)
    return lax.all_to_all(spread, axes, 0, 0).reshape(-1, L).astype(F32)


def on_device(
    latent, offset, owner, slot, cotangent, edge_in, edge_geo, edge_mid, edge_out, node_in, node_out, biases, ln_gain
):
    cells_x, cells_y, cap_size, width_l = cotangent.shape
    slots = cells_x * cells_y * cap_size
    width = cells_y + 2
    halo_rows = (cells_x + 2) * width * cap_size
    count_x = lax.axis_size("gx")
    count_y = lax.axis_size("gy")
    my_x = lax.axis_index("gx")
    my_y = lax.axis_index("gy")
    rows = latent.shape[0]
    send = rows // 9
    step_x = (owner // count_y - my_x + 1) % count_x
    step_y = (owner % count_y - my_y + 1) % count_y
    bucket = (step_x * 3 + step_y)[None, :]
    mark = slot + 1
    ones = jnp.ones((rows,), F32)
    zeros = jnp.zeros((rows,), F32)
    meta = jnp.stack(
        [
            offset[0].astype(F32), offset[1].astype(F32), ones, (mark // 16).astype(F32), (mark % 16).astype(F32),
            zeros, zeros, zeros,
        ]
    )
    (sent,) = call(sort_kernel, [((rows, 2 * L), BF)], [], latent, bucket, meta)
    sent = sent.reshape(3, 3, send, 2 * L)
    sections = [sent[:, 1], from_behind(sent[:, 2], "gy", 1), from_behind(sent[:, 0], "gy", -1)]
    section = jnp.stack(sections)
    final = [section[:, 1], from_behind(section[:, 2], "gx", 1), from_behind(section[:, 0], "gx", -1)]
    arrived = jnp.concatenate([piece.reshape(-1, 2 * L) for piece in final], axis=0)
    v0, own0, pay = call(
        place_kernel, [((slots, L), BF), ((slots, L), F32), ((slots, 2 * L), BF)], [], arrived, edge_in[0]
    )
    halo = with_halo(pay.reshape(cells_x, cells_y, cap_size, 2 * L)).reshape(halo_rows, 2 * L)

    def weights(t):
        return (edge_geo[t], edge_mid[t], edge_out[t], node_in[t], node_out[t], biases[t], ln_gain[t][None, :])

    node = ((slots, L), F32)
    node_low = ((slots, L), BF)
    geometry = [((EDGES, 2 * L), BF), ((EDGES, L), BF), ((L, EDGES), F32), ((L, EDGES), F32), ((80, EDGES), BF)]
    edge_scratch = [((halo_rows, L), F32), node, node]
    sums_scratch = [((2 * L, 2 * L), F32), ((96, 2 * L), F32), ((8, 2 * L), F32)]
    sums_scratch += [((2 * L, 2 * L), BF)] * 2 + [((8, L), F32)]
    firsts = call(
        functools.partial(first_kernel, width),
        geometry + [node_low, node, node_low, node, node_low, node_low, node, node_low, node, node],
        edge_scratch + [((2 * L, 2 * L), BF)],
        halo, pay, own0, v0, *weights(0), edge_in[1],
    )
    lhs, weight, weight_t, radius_t, hot_t = firsts[:5]
    v1, own1, far1 = firsts[5:8]
    saved0 = firsts[8:]
    far1_halo = with_halo(far1.reshape(cells_x, cells_y, cap_size, L)).reshape(halo_rows, L)
    edge_outs = [node, ((halo_rows, L), F32), node, ((768, L), F32)]
    v2, d_own1, d_far1, grad1, grads1 = call(
        functools.partial(middle_kernel, width),
        [node_low] + edge_outs,
        edge_scratch + [node] + sums_scratch,
        far1_halo, halo, pay, own1, v1, cotangent.reshape(slots, L), lhs, weight, weight_t, radius_t, hot_t, *weights(1),
    )
    d_far1 = fold_halo(d_far1.reshape(cells_x + 2, width, cap_size, L)).reshape(slots, L)
    d_own0, d_far0, grad0, grads0, grad_in1 = call(
        functools.partial(back_kernel, width),
        edge_outs + [((L, 2 * L), F32)],
        edge_scratch + sums_scratch,
        d_own1, d_far1, grad1, v1, edge_in[1], halo, pay, own0, v0, lhs, weight, radius_t, hot_t, *saved0, *weights(0),
    )
    d_far0 = fold_halo(d_far0.reshape(cells_x + 2, width, cap_size, L)).reshape(slots, L)
    latent_grad, grad_in0 = call(
        last_kernel, [node, ((L, 2 * L), F32)], [], d_own0, d_far0, grad0, v0, edge_in[0], pay
    )
    packed = jnp.concatenate(
        [
            grad_in0[:, :L], grad_in0[:, L:], grads0, grad_in1[:, :L], grad_in1[:, L:], grads1,
        ],
        axis=0,
    )
    total = total_over_devices(packed) * (float(slots * count_x * count_y) ** -0.5)
    total = total.reshape(STEPS, GROWS, L)
    cells = (cells_x, cells_y, cap_size, width_l)
    return (
        v2.reshape(cells),
        latent_grad.reshape(cells),
        jnp.concatenate([total[:, :L], total[:, L : 2 * L]], axis=2),
        total[:, 902:905],
        total[:, 2 * L : 3 * L],
        total[:, 3 * L : 4 * L],
        total[:, 4 * L : 6 * L],
        total[:, 6 * L : 7 * L],
        total[:, 896:901],
        total[:, 901],
    )


def solution(mesh):
    rows = P(("gx", "gy"))
    grid = P("gx", "gy", None, None)
    in_specs = (P(("gx", "gy"), None), P(None, ("gx", "gy")), rows, rows, grid) + (P(),) * 8
    out_specs = (grid, grid) + (P(),) * 8
    return jax.shard_map(on_device, mesh=mesh, in_specs=in_specs, out_specs=out_specs, check_vma=False)
```

profile of v0, /device:TPU:1, one launch (start us, length us, event | category | flops | bytes accessed | tf_op | source)
XLA Modules:
  0.0 201.9 jit_solution(1038345934234860972)
XLA Ops:
  0.7 0.7 copy-done.8
  1.3 0.7 copy-done.10
  2.0 0.7 copy-done.11
  2.8 0.9 copy-done.1
  4.3 2.2 %collective-permute-start = (bf16[3,48,256]{2,1,0:T(8,128)(2,1)S(1)}, bf16[3,48,256]{2,1,0:T(8,128)(2,1)S(1)}, u32[]{:S(2)}, u32[]{:S(2)}) collective-permute-start(bf16[3,48,256]{2,1,0:T(8,128)(2,1)S(1)} %get-tuple-element.111), channel_id=1, source_target_pairs={{0,1},{1,2},{2,3},{3,0},{4,5},{5,6},{6,7},{7,4},{8,9},{9,10},{10,1... | collective-permute-start | bytes 221192 | tf_op jit(solution)/shard_map/ppermute | solution.py:446
  6.5 2.1 %collective-permute-start.1 = (bf16[3,48,256]{2,1,0:T(8,128)(2,1)S(1)}, bf16[3,48,256]{2,1,0:T(8,128)(2,1)S(1)}, u32[]{:S(2)}, u32[]{:S(2)}) collective-permute-start(bf16[3,48,256]{2,1,0:T(8,128)(2,1)S(1)} %get-tuple-element.112), channel_id=1, source_target_pairs={{0,3},{1,0},{2,1},{3,2},{4,7},{5,4},{6,5},{7,6},{8,11},{9,8},{10,9... | collective-permute-start | bytes 221192 | tf_op jit(solution)/shard_map/ppermute | solution.py:446
  8.6 0.8 copy-done.5
  9.5 0.8 copy-done.4
  10.3 1.3 collective-permute-done.1
  11.7 1.1 collective-permute-start.3
  12.9 1.2 collective-permute-start.2
  14.0 2.0 collective-permute-done.3
  16.0 0.7 shard_map.205
  16.7 2.5 %collective-permute-start.4 = (bf16[1,8,8,256]{3,2,1,0:T(8,128)(2,1)S(1)}, bf16[1,8,8,256]{3,2,1,0:T(8,128)(2,1)S(1)}, u32[]{:S(2)}, u32[]{:S(2)}) collective-permute-start(bf16[1,8,8,256]{3,2,1,0:T(8,128)(2,1)S(1)} %get-tuple-element.105), channel_id=1, source_target_pairs={{0,4},{4,8},{8,12},{12,16},{16,20},{20,24},{24,28},{28,0},{1,5},{5... | collective-permute-start | bytes 98312 | tf_op jit(solution)/shard_map/ppermute | solution.py:446
  19.5 0.6 collective-permute-done.4
  20.2 2.3 %collective-permute-done.5 = bf16[1,8,8,256]{3,2,1,0:T(8,128)(2,1)S(1)} collective-permute-done((bf16[1,8,8,256]{3,2,1,0:T(8,128)(2,1)S(1)}, bf16[1,8,8,256]{3,2,1,0:T(8,128)(2,1)S(1)}, u32[]{:S(2)}, u32[]{:S(2)}) %collective-permute-start.5) | collective-permute-done | bytes 32800 | tf_op jit(solution)/shard_map/ppermute | solution.py:446
  22.9 2.9 %collective-permute-start.7 = (bf16[10,1,8,256]{3,2,1,0:T(8,128)(2,1)S(1)}, bf16[10,1,8,256]{3,2,1,0:T(8,128)(2,1)S(1)}, u32[]{:S(2)}, u32[]{:S(2)}) collective-permute-start(bf16[10,1,8,256]{3,2,1,0:T(8,128)(2,1)S(1)} %get-tuple-element.104), channel_id=1, source_target_pairs={{0,3},{1,0},{2,1},{3,2},{4,7},{5,4},{6,5},{7,6},{8,11},{9,8},{10,9... | collective-permute-start | bytes 122888 | tf_op jit(solution)/shard_map/ppermute | solution.py:446
  25.9 1.5 collective-permute-done.6
  27.4 19.9 %shard_map.206 = (bf16[576,256]{1,0:T(8,128)(2,1)S(1)}, bf16[576,128]{1,0:T(8,128)(2,1)S(1)}, f32[128,576]{1,0:T(8,128)S(1)}, f32[128,576]{1,0:T(8,128)S(1)}, bf...) custom-call(bf16[800,256]{1,0:T(8,128)(2,1)S(1)} %bitcast.97, ...), custom_call_target="tpu_custom_call" | custom-call | tf_op jit(solution)/shard_map/pallas_call | solution.py:434
  47.4 1.2 collective-permute-start.8
  48.6 1.6 collective-permute-start.9
  50.2 0.6 collective-permute-done.8
  50.8 0.9 collective-permute-done.9
  51.8 0.6 collective-permute-start.10
  52.4 3.1 %collective-permute-start.11 = (bf16[10,1,8,128]{3,2,1,0:T(8,128)(2,1)S(1)}, bf16[10,1,8,128]{3,2,1,0:T(8,128)(2,1)S(1)}, u32[]{:S(2)}, u32[]{:S(2)}) collective-permute-start(bf16[10,1,8,128]{3,2,1,0:T(8,128)(2,1)S(1)} %get-tuple-element.122), channel_id=1, source_target_pairs={{0,3},{1,0},{2,1},{3,2},{4,7},{5,4},{6,5},{7,6},{8,11},{9,8},{10,9... | collective-permute-start | bytes 61448 | tf_op jit(solution)/shard_map/ppermute | solution.py:446
  55.5 1.1 collective-permute-done.10
  56.7 48.6 %shard_map.207 = (bf16[512,128]{1,0:T(8,128)(2,1)}, f32[512,128]{1,0:T(8,128)S(1)}, f32[800,128]{1,0:T(8,128)S(1)}, f32[512,128]{1,0:T(8,128)S(1)}, f32[768,128]{1,0:T(8,128)S(1)}) custom-call(bf16[800,128]{1,0:T(8,128)(2,1)S(1)} %bitcast.103, bf16[800,256]{1,0:T(8,128)(2,1)S(1)} %bitcast.98, bf16[512,256]{1,0:T(8,128)(2,1)S(1)} %get-tuple-element.40.pay_ref, ...), custom_call_target="tpu_custom_call" | custom-call | tf_op jit(solution)/shard_map/pallas_call | solution.py:434
  105.3 1.5 collective-permute-start.12
  106.9 1.8 collective-permute-start.13
  108.7 0.6 collective-permute-done.12
  109.3 1.3 collective-permute-done.13
  111.2 2.8 %collective-permute-start.15 = (bf16[8,1,8,128]{3,2,1,0:T(8,128)(2,1)S(1)}, bf16[8,1,8,128]{3,2,1,0:T(8,128)(2,1)S(1)}, u32[]{:S(2)}, u32[]{:S(2)}) collective-permute-start(bf16[8,1,8,128]{3,2,1,0:T(8,128)(2,1)S(1)} %get-tuple-element.120), channel_id=1, source_target_pairs={{0,3},{1,0},{2,1},{3,2},{4,7},{5,4},{6,5},{7,6},{8,11},{9,8},{10,9... | collective-permute-start | bytes 49160 | tf_op jit(solution)/shard_map/ppermute | solution.py:446
  114.1 1.0 collective-permute-done.14
  115.1 29.8 %shard_map.208 = (f32[512,128]{1,0:T(8,128)S(1)}, f32[800,128]{1,0:T(8,128)S(1)}, f32[512,128]{1,0:T(8,128)S(1)}, f32[768,128]{1,0:T(8,128)S(1)}, f32[128,256]{1,0:T(8,128)S(1)}) custom-call(f32[512,128]{1,0:T(8,128)S(1)} %get-tuple-element.52.next_d_own_ref, f32[512,128]{1,0:T(8,128)S(1)} %bitcast.100, f32[512,128]{1,0:T(8,128)S(1)} %get-tuple-element.54.next_grad_ref, ...), custom_call_target="tpu_custom_call" | custom-call | tf_op jit(solution)/shard_map/pallas_call | solution.py:434
  145.0 1.6 collective-permute-start.16
  146.6 1.9 collective-permute-start.17
  148.5 0.6 collective-permute-done.16
  149.1 1.5 collective-permute-done.17
  150.7 0.6 collective-permute-start.18
  151.3 2.8 %collective-permute-start.19 = (bf16[8,1,8,128]{3,2,1,0:T(8,128)(2,1)S(1)}, bf16[8,1,8,128]{3,2,1,0:T(8,128)(2,1)S(1)}, u32[]{:S(2)}, u32[]{:S(2)}) collective-permute-start(bf16[8,1,8,128]{3,2,1,0:T(8,128)(2,1)S(1)} %get-tuple-element.118), channel_id=1, source_target_pairs={{0,3},{1,0},{2,1},{3,2},{4,7},{5,4},{6,5},{7,6},{8,11},{9,8},{10,9... | collective-permute-start | bytes 49160 | tf_op jit(solution)/shard_map/ppermute | solution.py:446
  154.2 1.0 collective-permute-done.18
  155.3 1.0 shard_map.209
  156.4 23.0 %all_to_all.10 = bf16[32,64,128]{2,1,0:T(8,128)(2,1)S(1)} all-to-all(bf16[32,64,128]{2,1,0:T(8,128)(2,1)S(1)} %bitcast.123), channel_id=1, replica_groups=mesh['gx'=8,'gy'=4] {'gx','gy'}, dimensions={0} | all-to-all | bytes 1048576 | tf_op jit(solution)/shard_map/all_to_all | solution.py:473
  179.6 18.2 %all_to_all.11 = bf16[32,64,128]{2,1,0:T(8,128)(2,1)S(1)} all-to-all(bf16[32,64,128]{2,1,0:T(8,128)(2,1)S(1)} %broadcast_in_dim.10), channel_id=1, replica_groups=mesh['gx'=8,'gy'=4] {'gx','gy'}, dimensions={0} | all-to-all | bytes 1048576 | tf_op jit(solution)/shard_map/all_to_all | solution.py:476
  198.6 0.7 slice.372
  199.3 0.8 fusion.14
  200.6 0.6 copy.43
  201.2 0.7 pad_maximum_fusion.5
  (93 shorter events, 4.3 us)
Async XLA Ops:
  0.6 0.7 copy-start.8
  1.3 0.7 copy-start.10
  2.0 0.7 copy-start.11
  2.8 0.9 copy-start.1
  4.3 4.3 %copy-start.2 = (bf16[2,128,256]{2,1,0:T(8,128)(2,1)S(1)}, bf16[2,128,256]{2,1,0:T(8,128)(2,1)}, u32[]{:S(2)}) copy-start(bf16[2,128,256]{2,1,0:T(8,128)(2,1)} %param.18) | copy-start | bytes 393220
  4.3 6.0 %collective-permute-start = (bf16[3,48,256]{2,1,0:T(8,128)(2,1)S(1)}, bf16[3,48,256]{2,1,0:T(8,128)(2,1)S(1)}, u32[]{:S(2)}, u32[]{:S(2)}) collective-permute-start(bf16[3,48,256]{2,1,0:T(8,128)(2,1)S(1)} %get-tuple-element.111), channel_id=1, source_target_pairs={{0,1},{1,2},{2,3},{3,0},{4,5},{5,6},{6,7},{7,4},{8,9},{9,10},{10,1... | collective-permute-start | bytes 221192 | tf_op jit(solution)/shard_map/ppermute | solution.py:446
  6.5 2.1 %copy-start.3 = (bf16[2,256,128]{2,1,0:T(8,128)(2,1)S(1)}, bf16[2,256,128]{2,1,0:T(8,128)(2,1)}, u32[]{:S(2)}) copy-start(bf16[2,256,128]{2,1,0:T(8,128)(2,1)} %param.22) | copy-start | bytes 393220
  6.5 5.2 %collective-permute-start.1 = (bf16[3,48,256]{2,1,0:T(8,128)(2,1)S(1)}, bf16[3,48,256]{2,1,0:T(8,128)(2,1)S(1)}, u32[]{:S(2)}, u32[]{:S(2)}) collective-permute-start(bf16[3,48,256]{2,1,0:T(8,128)(2,1)S(1)} %get-tuple-element.112), channel_id=1, source_target_pairs={{0,3},{1,0},{2,1},{3,2},{4,7},{5,4},{6,5},{7,6},{8,11},{9,8},{10,9... | collective-permute-start | bytes 221192 | tf_op jit(solution)/shard_map/ppermute | solution.py:446
  8.6 0.8 copy-start.5
  8.6 0.9 copy-start.6
  9.5 0.8 copy-start.4
  11.7 2.3 %copy-start.7 = (bf16[2,5,128]{2,0,1:T(2,128)(2,1)S(1)}, bf16[2,5,128]{2,0,1:T(2,128)(2,1)}, u32[]{:S(2)}) copy-start(bf16[2,5,128]{2,0,1:T(2,128)(2,1)} %param.24) | copy-start | bytes 7684
  11.7 4.2 %collective-permute-start.3 = (bf16[3,48,256]{2,1,0:T(8,128)(2,1)S(1)}, bf16[3,48,256]{2,1,0:T(8,128)(2,1)S(1)}, u32[]{:S(2)}, u32[]{:S(2)}) collective-permute-start(bf16[3,48,256]{2,1,0:T(8,128)(2,1)S(1)} %get-tuple-element.108), channel_id=1, source_target_pairs={{0,28},{4,0},{8,4},{12,8},{16,12},{20,16},{24,20},{28,24},{1,29},{... | collective-permute-start | bytes 221192 | tf_op jit(solution)/shard_map/ppermute | solution.py:446
  12.9 3.1 %collective-permute-start.2 = (bf16[3,48,256]{2,1,0:T(8,128)(2,1)S(1)}, bf16[3,48,256]{2,1,0:T(8,128)(2,1)S(1)}, u32[]{:S(2)}, u32[]{:S(2)}) collective-permute-start(bf16[3,48,256]{2,1,0:T(8,128)(2,1)S(1)} %get-tuple-element.109), channel_id=1, source_target_pairs={{0,4},{4,8},{8,12},{12,16},{16,20},{20,24},{24,28},{28,0},{1,5},{5... | collective-permute-start | bytes 221192 | tf_op jit(solution)/shard_map/ppermute | solution.py:446
  16.7 2.8 %copy-start.9 = (bf16[2,3,128]{2,0,1:T(2,128)(2,1)S(1)}, bf16[2,3,128]{2,0,1:T(2,128)(2,1)}, u32[]{:S(2)}) copy-start(bf16[2,3,128]{2,0,1:T(2,128)(2,1)} %param.19) | copy-start | bytes 4612
  16.7 3.5 %collective-permute-start.4 = (bf16[1,8,8,256]{3,2,1,0:T(8,128)(2,1)S(1)}, bf16[1,8,8,256]{3,2,1,0:T(8,128)(2,1)S(1)}, u32[]{:S(2)}, u32[]{:S(2)}) collective-permute-start(bf16[1,8,8,256]{3,2,1,0:T(8,128)(2,1)S(1)} %get-tuple-element.105), channel_id=1, source_target_pairs={{0,4},{4,8},{8,12},{12,16},{16,20},{20,24},{24,28},{28,0},{1,5},{5... | collective-permute-start | bytes 98312 | tf_op jit(solution)/shard_map/ppermute | solution.py:446
  19.2 3.3 %collective-permute-start.5 = (bf16[1,8,8,256]{3,2,1,0:T(8,128)(2,1)S(1)}, bf16[1,8,8,256]{3,2,1,0:T(8,128)(2,1)S(1)}, u32[]{:S(2)}, u32[]{:S(2)}) collective-permute-start(bf16[1,8,8,256]{3,2,1,0:T(8,128)(2,1)S(1)} %get-tuple-element.106), channel_id=1, source_target_pairs={{0,28},{4,0},{8,4},{12,8},{16,12},{20,16},{24,20},{28,24},{1,29},{... | collective-permute-start | bytes 98312 | tf_op jit(solution)/shard_map/ppermute | solution.py:446
  22.5 3.3 %copy-start.12 = (bf16[2,128]{1,0:T(2,128)(2,1)S(1)}, bf16[2,128]{1,0:T(2,128)(2,1)}, u32[]{:S(2)}) copy-start(bf16[2,128]{1,0:T(2,128)(2,1)} %param.25) | copy-start | bytes 1540
  22.5 4.8 %collective-permute-start.6 = (bf16[10,1,8,256]{3,2,1,0:T(8,128)(2,1)S(1)}, bf16[10,1,8,256]{3,2,1,0:T(8,128)(2,1)S(1)}, u32[]{:S(2)}, u32[]{:S(2)}) collective-permute-start(bf16[10,1,8,256]{3,2,1,0:T(8,128)(2,1)S(1)} %get-tuple-element.103), channel_id=1, source_target_pairs={{0,1},{1,2},{2,3},{3,0},{4,5},{5,6},{6,7},{7,4},{8,9},{9,10},{10,1... | collective-permute-start | bytes 122888 | tf_op jit(solution)/shard_map/ppermute | solution.py:446
  22.9 4.4 %collective-permute-start.7 = (bf16[10,1,8,256]{3,2,1,0:T(8,128)(2,1)S(1)}, bf16[10,1,8,256]{3,2,1,0:T(8,128)(2,1)S(1)}, u32[]{:S(2)}, u32[]{:S(2)}) collective-permute-start(bf16[10,1,8,256]{3,2,1,0:T(8,128)(2,1)S(1)} %get-tuple-element.104), channel_id=1, source_target_pairs={{0,3},{1,0},{2,1},{3,2},{4,7},{5,4},{6,5},{7,6},{8,11},{9,8},{10,9... | collective-permute-start | bytes 122888 | tf_op jit(solution)/shard_map/ppermute | solution.py:446
  47.4 3.4 %collective-permute-start.8 = (bf16[1,8,8,128]{3,2,1,0:T(8,128)(2,1)S(1)}, bf16[1,8,8,128]{3,2,1,0:T(8,128)(2,1)S(1)}, u32[]{:S(2)}, u32[]{:S(2)}) collective-permute-start(bf16[1,8,8,128]{3,2,1,0:T(8,128)(2,1)S(1)} %get-tuple-element.125), channel_id=1, source_target_pairs={{0,4},{4,8},{8,12},{12,16},{16,20},{20,24},{24,28},{28,0},{1,5},{5... | collective-permute-start | bytes 49160 | tf_op jit(solution)/shard_map/ppermute | solution.py:446
  48.6 3.2 %collective-permute-start.9 = (bf16[1,8,8,128]{3,2,1,0:T(8,128)(2,1)S(1)}, bf16[1,8,8,128]{3,2,1,0:T(8,128)(2,1)S(1)}, u32[]{:S(2)}, u32[]{:S(2)}) collective-permute-start(bf16[1,8,8,128]{3,2,1,0:T(8,128)(2,1)S(1)} %get-tuple-element.126), channel_id=1, source_target_pairs={{0,28},{4,0},{8,4},{12,8},{16,12},{20,16},{24,20},{28,24},{1,29},{... | collective-permute-start | bytes 49160 | tf_op jit(solution)/shard_map/ppermute | solution.py:446
  51.8 4.8 %collective-permute-start.10 = (bf16[10,1,8,128]{3,2,1,0:T(8,128)(2,1)S(1)}, bf16[10,1,8,128]{3,2,1,0:T(8,128)(2,1)S(1)}, u32[]{:S(2)}, u32[]{:S(2)}) collective-permute-start(bf16[10,1,8,128]{3,2,1,0:T(8,128)(2,1)S(1)} %get-tuple-element.121), channel_id=1, source_target_pairs={{0,1},{1,2},{2,3},{3,0},{4,5},{5,6},{6,7},{7,4},{8,9},{9,10},{10,1... | collective-permute-start | bytes 61448 | tf_op jit(solution)/shard_map/ppermute | solution.py:446
  52.4 4.2 %collective-permute-start.11 = (bf16[10,1,8,128]{3,2,1,0:T(8,128)(2,1)S(1)}, bf16[10,1,8,128]{3,2,1,0:T(8,128)(2,1)S(1)}, u32[]{:S(2)}, u32[]{:S(2)}) collective-permute-start(bf16[10,1,8,128]{3,2,1,0:T(8,128)(2,1)S(1)} %get-tuple-element.122), channel_id=1, source_target_pairs={{0,3},{1,0},{2,1},{3,2},{4,7},{5,4},{6,5},{7,6},{8,11},{9,8},{10,9... | collective-permute-start | bytes 61448 | tf_op jit(solution)/shard_map/ppermute | solution.py:446
  55.5 1.2 copy-start
  105.3 4.0 %collective-permute-start.12 = (bf16[1,10,8,128]{3,2,1,0:T(8,128)(2,1)S(1)}, bf16[1,10,8,128]{3,2,1,0:T(8,128)(2,1)S(1)}, u32[]{:S(2)}, u32[]{:S(2)}) collective-permute-start(bf16[1,10,8,128]{3,2,1,0:T(8,128)(2,1)S(1)} %get-tuple-element.115), channel_id=1, source_target_pairs={{0,4},{4,8},{8,12},{12,16},{16,20},{20,24},{24,28},{28,0},{1,5},{5... | collective-permute-start | bytes 61448 | tf_op jit(solution)/shard_map/ppermute | solution.py:446
  106.9 3.7 %collective-permute-start.13 = (bf16[1,10,8,128]{3,2,1,0:T(8,128)(2,1)S(1)}, bf16[1,10,8,128]{3,2,1,0:T(8,128)(2,1)S(1)}, u32[]{:S(2)}, u32[]{:S(2)}) collective-permute-start(bf16[1,10,8,128]{3,2,1,0:T(8,128)(2,1)S(1)} %get-tuple-element.116), channel_id=1, source_target_pairs={{0,28},{4,0},{8,4},{12,8},{16,12},{20,16},{24,20},{28,24},{1,29},{... | collective-permute-start | bytes 61448 | tf_op jit(solution)/shard_map/ppermute | solution.py:446
  110.6 4.4 %collective-permute-start.14 = (bf16[8,1,8,128]{3,2,1,0:T(8,128)(2,1)S(1)}, bf16[8,1,8,128]{3,2,1,0:T(8,128)(2,1)S(1)}, u32[]{:S(2)}, u32[]{:S(2)}) collective-permute-start(bf16[8,1,8,128]{3,2,1,0:T(8,128)(2,1)S(1)} %get-tuple-element.119), channel_id=1, source_target_pairs={{0,1},{1,2},{2,3},{3,0},{4,5},{5,6},{6,7},{7,4},{8,9},{9,10},{10,1... | collective-permute-start | bytes 49160 | tf_op jit(solution)/shard_map/ppermute | solution.py:446
  111.2 3.9 %collective-permute-start.15 = (bf16[8,1,8,128]{3,2,1,0:T(8,128)(2,1)S(1)}, bf16[8,1,8,128]{3,2,1,0:T(8,128)(2,1)S(1)}, u32[]{:S(2)}, u32[]{:S(2)}) collective-permute-start(bf16[8,1,8,128]{3,2,1,0:T(8,128)(2,1)S(1)} %get-tuple-element.120), channel_id=1, source_target_pairs={{0,3},{1,0},{2,1},{3,2},{4,7},{5,4},{6,5},{7,6},{8,11},{9,8},{10,9... | collective-permute-start | bytes 49160 | tf_op jit(solution)/shard_map/ppermute | solution.py:446
  145.0 4.1 %collective-permute-start.16 = (bf16[1,10,8,128]{3,2,1,0:T(8,128)(2,1)S(1)}, bf16[1,10,8,128]{3,2,1,0:T(8,128)(2,1)S(1)}, u32[]{:S(2)}, u32[]{:S(2)}) collective-permute-start(bf16[1,10,8,128]{3,2,1,0:T(8,128)(2,1)S(1)} %get-tuple-element.113), channel_id=1, source_target_pairs={{0,4},{4,8},{8,12},{12,16},{16,20},{20,24},{24,28},{28,0},{1,5},{5... | collective-permute-start | bytes 61448 | tf_op jit(solution)/shard_map/ppermute | solution.py:446
  146.6 4.0 %collective-permute-start.17 = (bf16[1,10,8,128]{3,2,1,0:T(8,128)(2,1)S(1)}, bf16[1,10,8,128]{3,2,1,0:T(8,128)(2,1)S(1)}, u32[]{:S(2)}, u32[]{:S(2)}) collective-permute-start(bf16[1,10,8,128]{3,2,1,0:T(8,128)(2,1)S(1)} %get-tuple-element.114), channel_id=1, source_target_pairs={{0,28},{4,0},{8,4},{12,8},{16,12},{20,16},{24,20},{28,24},{1,29},{... | collective-permute-start | bytes 61448 | tf_op jit(solution)/shard_map/ppermute | solution.py:446
  150.7 4.5 %collective-permute-start.18 = (bf16[8,1,8,128]{3,2,1,0:T(8,128)(2,1)S(1)}, bf16[8,1,8,128]{3,2,1,0:T(8,128)(2,1)S(1)}, u32[]{:S(2)}, u32[]{:S(2)}) collective-permute-start(bf16[8,1,8,128]{3,2,1,0:T(8,128)(2,1)S(1)} %get-tuple-element.117), channel_id=1, source_target_pairs={{0,1},{1,2},{2,3},{3,0},{4,5},{5,6},{6,7},{7,4},{8,9},{9,10},{10,1... | collective-permute-start | bytes 49160 | tf_op jit(solution)/shard_map/ppermute | solution.py:446
  151.3 3.9 %collective-permute-start.19 = (bf16[8,1,8,128]{3,2,1,0:T(8,128)(2,1)S(1)}, bf16[8,1,8,128]{3,2,1,0:T(8,128)(2,1)S(1)}, u32[]{:S(2)}, u32[]{:S(2)}) collective-permute-start(bf16[8,1,8,128]{3,2,1,0:T(8,128)(2,1)S(1)} %get-tuple-element.118), channel_id=1, source_target_pairs={{0,3},{1,0},{2,1},{3,2},{4,7},{5,4},{6,5},{7,6},{8,11},{9,8},{10,9... | collective-permute-start | bytes 49160 | tf_op jit(solution)/shard_map/ppermute | solution.py:446
where the time goes:
time: 202 us
  Pallas kernels  101 us (50%)
  blocking collectives  41.3 us (20%)
  starting transfers between devices  32.9 us (16%)
  waiting for transfers between devices  16.4 us (8%)
  local copies, waits for them, and re-layouts  8.22 us (4%)
    pallas_call x6, Pallas kernels, call(): pl.pallas_call(kernel, out_shape=[jax.ShapeDtypeStruct(shape, dtype) for...  101 us
    ppermute x20, starting transfers between devices, from_behind(): lax.ppermute(value, axis, [(source, (source + steps) % count) for source...  32.9 us
    all_to_all x1, blocking collectives, total_over_devices(): parts = lax.all_to_all(rows.astype(BF).reshape(count, -1, L), axes, 0, 0)  23 us
    all_to_all x1, blocking collectives, total_over_devices(): return lax.all_to_all(spread, axes, 0, 0).reshape(-1, L).astype(F32)  18.2 us
    ppermute x20, waiting for transfers between devices, from_behind(): lax.ppermute(value, axis, [(source, (source + steps) % count) for source...  16.4 us
    unnamed x36, local copies, waits for them, and re-layouts  5.83 us
  transfers between devices with their start and end apart: 20, of which 14 were waited for; matrix products, arithmetic and copies ran while one was open for 0% of the time, Pallas kernels for 0%

commit v1 on v0

--- a/solution.py
+++ b/solution.py
@@ -59,20 +59,14 @@
     out_ref[:, L:] = dot_nt(perm, meta).astype(BF)
 
 
-def place_kernel(rows_ref, edge_in_ref, latent_ref, own_ref, pay_ref):
+def place_kernel(rows_ref, pay_ref):
     rows = rows_ref.shape[0]
-    slots = latent_ref.shape[0]
+    slots = pay_ref.shape[0]
     pick_lane = iota((8, L), 1)
     pick = jnp.where(pick_lane == 3, 16.0, jnp.where(pick_lane == 4, 1.0, 0.0)).astype(BF)
     mark = dot_nt(pick, rows_ref[:, L:])[0:1]
     hot = mask((iota((slots, rows), 0) + 1).astype(F32) == mark).astype(BF)
-    placed = dot(hot, rows_ref[...]).astype(BF)
-    latent = placed[:, :L]
-    latent_ref[...] = latent
-    both = dot(latent, edge_in_ref[...])
-    own_ref[...] = both[:, :L]
-    pay_ref[:, :L] = both[:, L:].astype(BF)
-    pay_ref[:, L:] = placed[:, L:]
+    pay_ref[...] = dot(hot, rows_ref[...]).astype(BF)
 
 
 def fill_geometry(geo, width, lhs_ref, weight_ref, weight_t_ref, radius_t_ref, hot_t_ref):
@@ -181,7 +175,9 @@
     return ref[pl.ds(first, 1), :], ref[pl.ds(first + 1, 1), :]
 
 
-def edges_forward(width, lhs_ref, weight_t_ref, far_ref, near_ref, shifts, g2, mid2_ref, bias2, sums_ref, wsum_ref):
+def edges_forward(
+    width, lhs_ref, weight_t_ref, far_ref, near_ref, shifts, g2, mid2_ref, bias2, sums_ref, wsum_ref, keep=None
+):
     pairs = sums_ref.shape[0] // (2 * CAP)
     col = iota((CAP, EDGES), 1)
     start = iota((CAP, EDGES), 0) * NEAR
@@ -189,10 +185,17 @@
 
     def body(pair, carry):
         rhs = pair_rhs(pair, width, far_ref, near_ref, shifts, g2)
-        pre_one = dot(lhs_ref[...], rhs)
-        hidden = (pre_one + pre_one * jnp.tanh(pre_one)).astype(BF)
-        pre_two = dot(hidden, mid2_ref[...]) + bias2
-        act = (pre_two + pre_two * jnp.tanh(pre_two)).astype(BF)
+        pre_one = dot(lhs_ref[...], rhs).astype(BF)
+        tanh_one = jnp.tanh(pre_one)
+        hidden = pre_one + pre_one * tanh_one
+        pre_two = (dot(hidden, mid2_ref[...]) + bias2).astype(BF)
+        tanh_two = jnp.tanh(pre_two)
+        act = pre_two + pre_two * tanh_two
+        if keep is not None:
+            at = pl.ds(pl.multiple_of(pair * EDGES, EDGES), EDGES)
+            keep[0][at, :] = hidden
+            keep[1][at, :] = slope_of(pre_one, tanh_one)
+            keep[2][at, :] = slope_of(pre_two, tanh_two)
         row_a, row_b = pair_rows(pair, width, weight_t_ref)
         spread = jnp.concatenate([own * row_a, own * row_b], axis=0)
         sums = dot(spread.astype(BF), act)
@@ -201,37 +204,41 @@
         wsum_ref[at, :] = jnp.broadcast_to(jnp.sum(spread, axis=1, keepdims=True), (2 * CAP, L))
         return carry
 
-    lax.fori_loop(0, pairs, body, 0)
+    lax.fori_loop(0, pairs, body, 0, unroll=4)
 
 
 def edges_backward(
     width, lhs_ref, weight_ref, radius_t_ref, hot_t_ref, far_ref, near_ref, shifts, g2, mid2_ref, mid2_t_ref, bias2,
-    d_sums_ref, d_own_ref, d_far_ref, mid_ref, rows_ref, bias_ref,
+    d_sums_ref, d_own_ref, d_far_ref, mid_ref, rows_ref, bias_ref, keep=None,
 ):
     pairs = d_own_ref.shape[0] // (2 * CAP)
-    d_far_ref[...] = jnp.zeros_like(d_far_ref)
-    mid_ref[...] = jnp.zeros_like(mid_ref)
-    rows_ref[...] = jnp.zeros_like(rows_ref)
-    bias_ref[...] = jnp.zeros_like(bias_ref)
+    for ref in (d_far_ref, mid_ref, rows_ref, bias_ref):
+        ref[...] = jnp.zeros_like(ref)
 
     def body(pair, carry):
         x, y = pair_place(pair, width - 2)
-        rhs = pair_rhs(pair, width, far_ref, near_ref, shifts, g2)
-        pre_one = dot(lhs_ref[...], rhs)
-        tanh_one = jnp.tanh(pre_one)
-        hidden = (pre_one + pre_one * tanh_one).astype(BF)
-        pre_two = dot(hidden, mid2_ref[...]) + bias2
+        if keep is None:
+            rhs = pair_rhs(pair, width, far_ref, near_ref, shifts, g2)
+            pre_one = dot(lhs_ref[...], rhs).astype(BF)
+            tanh_one = jnp.tanh(pre_one)
+            hidden = pre_one + pre_one * tanh_one
+            pre_two = (dot(hidden, mid2_ref[...]) + bias2).astype(BF)
+            slope_one = slope_of(pre_one, tanh_one)
+            slope_two = slope_of(pre_two, jnp.tanh(pre_two))
+        else:
+            at = pl.ds(pl.multiple_of(pair * EDGES, EDGES), EDGES)
+            hidden, slope_one, slope_two = (ref[at, :] for ref in keep)
         pick = mask(pair_hot(pair, width)).astype(BF)
         weight = dot(weight_ref[...], pick)
         base = pl.multiple_of(pair * 2 * CAP, 2 * CAP)
         d_sums = d_sums_ref[pl.ds(base, 2 * CAP), :]
         d_sums = jnp.concatenate([d_sums[:CAP], d_sums[CAP:]], axis=1)
         d_sums = jnp.broadcast_to(d_sums[:, None, :], (CAP, NEAR, 2 * L)).reshape(EDGES, 2 * L)
-        d_two = weight * d_sums * slope_of(pre_two, jnp.tanh(pre_two))
+        d_two = weight * d_sums * slope_two
         bias_ref[...] += jnp.sum(d_two.reshape(EDGES // 8, 8, 2 * L), axis=0)
         d_two = d_two.astype(BF)
         mid_ref[...] += dot_tn(hidden, d_two)
-        d_one = (dot(d_two, mid2_t_ref[...]) * slope_of(pre_one, tanh_one)).astype(BF)
+        d_one = (dot(d_two, mid2_t_ref[...]) * slope_one).astype(BF)
         rad_a, rad_b = pair_rows(pair, width, radius_t_ref)
         tail = jnp.concatenate([rad_a, rad_b, jnp.zeros((14, EDGES), F32)], axis=0).astype(BF)
         back = dot(jnp.concatenate([hot_t_ref[...], tail], axis=0), d_one)
@@ -246,7 +253,7 @@
             d_far_ref[at, :] += both
         return carry
 
-    lax.fori_loop(0, pairs, body, 0)
+    lax.fori_loop(0, pairs, body, 0, unroll=4)
 
 
 def geo_grads(rows, d_far, geo_halo, d_own, geo_own):
@@ -309,135 +316,166 @@
 
 
 def store_node_grads(grads_ref, small_ref, grad_out, grad_first, grad_second, small):
-    base = L
+    base = 3 * L
     for block in (grad_out, grad_first[0], grad_first[1], grad_second):
-        grads_ref[base : base + L, :] = block
+        grads_ref[base : base + L, :] = block.astype(BF)
         base += L
     small_ref[...] = jnp.concatenate(small + [jnp.zeros((3, L), F32)], axis=0)
 
 
-def store_edge_grads(grads_ref, small_ref, mid, bias, geo):
-    grads_ref[:L, :] = mid[:L, :L] + mid[L:, L:]
+def store_edge_grads(grads_ref, small_ref, latent, latent_halo, d_own, d_far, mid, bias, geo):
+    grads_ref[:L, :] = dot_tn(latent, d_own.astype(BF)).astype(BF)
+    grads_ref[L : 2 * L, :] = dot_tn(latent_halo, d_far.astype(BF)).astype(BF)
+    grads_ref[2 * L : 3 * L, :] = (mid[:L, :L] + mid[L:, L:]).astype(BF)
     bias = jnp.sum(bias, axis=0, keepdims=True)
     rows = [bias[:, :L] + bias[:, L:], small_ref[:5, :]] + list(geo)
-    grads_ref[5 * L :, :] = jnp.concatenate(rows + [jnp.zeros((L - 9, L), F32)], axis=0)
-
-
-def edge_constants(edge_geo_ref, mid_ref, biases_ref, mid2_ref, mid2_t_ref=None):
-    edge_geo = edge_geo_ref[...]
-    mid = mid_ref[...].astype(F32)
-    mid2 = block_diag(0.5 * mid).astype(BF)
-    bias2 = twice(0.5 * biases_ref[0:1, :].astype(F32))
-    g2 = twice(0.5 * edge_geo[2:3].astype(F32))
-    mid2_ref[...] = mid2
+    grads_ref[7 * L :, :] = jnp.concatenate(rows + [jnp.zeros((L - 9, L), F32)], axis=0).astype(BF)
+
+
+class Step:
+    def __init__(self, refs, t):
+        names = ("edge_in", "edge_geo", "edge_mid", "edge_out", "node_in", "node_out", "biases")
+        for name, ref in zip(names, refs):
+            setattr(self, name, ref[t])
+        self.gain = refs[7][t : t + 1, :]
+
+
+def prepare(w, latent_halo, geo_halo, latent, geo_own, far_ref, near_ref, mid2_ref, mid2_t_ref=None):
+    far = dot(latent_halo, w.edge_in[:, L:]).astype(BF)
+    own = dot(latent, w.edge_in[:, :L])
+    fill_pre(far, geo_halo, own, geo_own, w.edge_geo, far_ref, near_ref)
+    mid = w.edge_mid.astype(F32)
+    mid2_ref[...] = block_diag(0.5 * mid).astype(BF)
     if mid2_t_ref is not None:
         mid2_t_ref[...] = block_diag(mid.T).astype(BF)
-    return shift_rows(edge_geo), g2, bias2
-
-
-def first_kernel(
-    width, halo_ref, pay_ref, own_ref, latent_ref, edge_geo_ref, mid_w_ref, out_w_ref, first_w_ref, second_w_ref,
-    biases_ref, gain_ref, next_in_ref,
-    lhs_ref, weight_ref, weight_t_ref, radius_t_ref, hot_t_ref, new_ref, next_own_ref, next_far_ref,
-    wsum_ref, sums_low_ref, message_ref, half_ref, first_low_ref, normed_ref, inv_ref,
-    far_ref, near_ref, sums_ref, mid2_ref,
-):
+    bias2 = twice(0.5 * w.biases[0:1].astype(F32))
+    g2 = twice(0.5 * w.edge_geo[2:3].astype(F32))
+    return shift_rows(w.edge_geo), g2, bias2
+
+
+def first_kernel(width, halo_ref, pay_ref, *refs):
+    w = Step(refs[:8], 0)
+    lhs_ref, weight_ref, weight_t_ref, radius_t_ref, hot_t_ref, new_ref, wsum_ref = refs[8:15]
+    saved_refs = refs[15:20]
+    inv_ref, far_ref, near_ref, sums_ref, mid2_ref = refs[20:]
     fill_geometry(halo_ref[:, L:], width, lhs_ref, weight_ref, weight_t_ref, radius_t_ref, hot_t_ref)
-    fill_pre(halo_ref[:, :L], halo_ref[:, L:], own_ref[...], pay_ref[:, L:], edge_geo_ref[...], far_ref, near_ref)
-    shifts, g2, bias2 = edge_constants(edge_geo_ref, mid_w_ref, biases_ref, mid2_ref)
+    latent, geo_own = pay_ref[:, :L], pay_ref[:, L:]
+    shifts, g2, bias2 = prepare(
+        w, halo_ref[:, :L], halo_ref[:, L:], latent, geo_own, far_ref, near_ref, mid2_ref
+    )
     edges_forward(width, lhs_ref, weight_t_ref, far_ref, near_ref, shifts, g2, mid2_ref, bias2, sums_ref, wsum_ref)
-    occ = column(pay_ref[:, L:], 2)
     new, saved = node_forward(
-        latent_ref[...], occ, sums_ref[...], wsum_ref[...], out_w_ref[...], first_w_ref[...], second_w_ref[...],
-        biases_ref[...], gain_ref[...],
-    )
-    for ref, value in zip((sums_low_ref, message_ref, half_ref, first_low_ref, normed_ref), saved):
+        pay_ref[:, :L], column(pay_ref[:, L:], 2), sums_ref[...], wsum_ref[...], w.edge_out, w.node_in, w.node_out,
+        w.biases, w.gain,
+    )
+    for ref, value in zip(saved_refs, saved):
         ref[...] = value
     inv_ref[...] = jnp.broadcast_to(saved[5], inv_ref.shape)
     new_ref[...] = new
-    both = dot(new, next_in_ref[...])
-    next_own_ref[...] = both[:, :L]
-    next_far_ref[...] = both[:, L:].astype(BF)
-
-
-def middle_kernel(
-    width, far_in_ref, halo_ref, pay_ref, own_ref, latent_ref, cot_ref, lhs_ref, weight_ref, weight_t_ref,
-    radius_t_ref, hot_t_ref, edge_geo_ref, mid_w_ref, out_w_ref, first_w_ref, second_w_ref, biases_ref, gain_ref,
-    new_ref, d_own_ref, d_far_ref, grad_ref, grads_ref,
-    far_ref, near_ref, sums_ref, wsum_ref, mid_ref, rows_ref, bias_ref, mid2_ref, mid2_t_ref, small_ref,
+
+
+def backward(
+    width, w, d_new, latent_halo_ref, latent_ref, halo_ref, pay_ref, saved, wsum_ref, geometry, consts, outs, scratch, keep
 ):
-    fill_pre(far_in_ref[...], halo_ref[:, L:], own_ref[...], pay_ref[:, L:], edge_geo_ref[...], far_ref, near_ref)
-    shifts, g2, bias2 = edge_constants(edge_geo_ref, mid_w_ref, biases_ref, mid2_ref, mid2_t_ref)
-    edges_forward(width, lhs_ref, weight_t_ref, far_ref, near_ref, shifts, g2, mid2_ref, bias2, sums_ref, wsum_ref)
-    occ = column(pay_ref[:, L:], 2)
-    new, saved = node_forward(
-        latent_ref[...], occ, sums_ref[...], wsum_ref[...], out_w_ref[...], first_w_ref[...], second_w_ref[...],
-        biases_ref[...], gain_ref[...],
-    )
-    new_ref[...] = new
-    d_new = cot_ref[...].astype(F32)
+    lhs_ref, weight_ref, radius_t_ref, hot_t_ref = geometry
+    d_own_ref, d_far_ref, grad_ref, grads_ref = outs
+    far_ref, near_ref, sums_ref, mid_ref, rows_ref, bias_ref, mid2_ref, mid2_t_ref, small_ref = scratch
+    shifts, g2, bias2 = consts
     d_sums, d_latent, grad_out, grad_first, grad_second, small = node_backward(
-        d_new, latent_ref[...], occ, wsum_ref[...], saved, out_w_ref[...], first_w_ref[...], second_w_ref[...],
-        gain_ref[...],
+        d_new, latent_ref[:, :L], column(pay_ref[:, L:], 2), wsum_ref[...], saved, w.edge_out, w.node_in, w.node_out,
+        w.gain,
     )
     sums_ref[...] = d_sums
     grad_ref[...] = d_new + d_latent
     store_node_grads(grads_ref, small_ref, grad_out, grad_first, grad_second, small)
     edges_backward(
         width, lhs_ref, weight_ref, radius_t_ref, hot_t_ref, far_ref, near_ref, shifts, g2, mid2_ref, mid2_t_ref, bias2,
-        sums_ref, d_own_ref, d_far_ref, mid_ref, rows_ref, bias_ref,
+        sums_ref, d_own_ref, d_far_ref, mid_ref, rows_ref, bias_ref, keep,
     )
     geo = geo_grads(rows_ref[...], d_far_ref[...], halo_ref[:, L:], d_own_ref[...], pay_ref[:, L:])
-    store_edge_grads(grads_ref, small_ref, mid_ref[...], bias_ref[...], geo)
-
-
-def back_kernel(
-    width, next_d_own_ref, next_d_far_ref, next_grad_ref, next_latent_ref, next_in_ref, halo_ref, pay_ref, own_ref,
-    latent_ref, lhs_ref, weight_ref, radius_t_ref, hot_t_ref, wsum_ref, sums_low_ref, message_ref, half_ref,
-    first_low_ref, normed_ref, inv_ref,
-    edge_geo_ref, mid_w_ref, out_w_ref, first_w_ref, second_w_ref, biases_ref, gain_ref,
-    d_own_ref, d_far_ref, grad_ref, grads_ref, grad_in_ref,
-    far_ref, near_ref, sums_ref, mid_ref, rows_ref, bias_ref, mid2_ref, mid2_t_ref, small_ref,
-):
+    store_edge_grads(
+        grads_ref, small_ref, latent_ref[:, :L], latent_halo_ref[:, :L], d_own_ref[...], d_far_ref[...], mid_ref[...],
+        bias_ref[...], geo,
+    )
+
+
+def middle_kernel(width, latent_halo_ref, halo_ref, pay_ref, latent_ref, cot_ref, *refs):
+    lhs_ref, weight_ref, weight_t_ref, radius_t_ref, hot_t_ref = refs[:5]
+    w = Step(refs[5:13], 1)
+    new_ref = refs[13]
+    outs = refs[14:18]
+    scratch = refs[18:27]
+    wsum_ref = refs[27]
+    keep = refs[28:]
+    far_ref, near_ref, sums_ref = scratch[:3]
+    mid2_ref, mid2_t_ref = scratch[6:8]
+    consts = prepare(
+        w, latent_halo_ref[...], halo_ref[:, L:], latent_ref[...], pay_ref[:, L:], far_ref, near_ref, mid2_ref, mid2_t_ref
+    )
+    shifts, g2, bias2 = consts
+    edges_forward(
+        width, lhs_ref, weight_t_ref, far_ref, near_ref, shifts, g2, mid2_ref, bias2, sums_ref, wsum_ref, keep
+    )
+    new, saved = node_forward(
+        latent_ref[...], column(pay_ref[:, L:], 2), sums_ref[...], wsum_ref[...], w.edge_out, w.node_in, w.node_out,
+        w.biases, w.gain,
+    )
+    new_ref[...] = new
+    backward(
+        width, w, cot_ref[...].astype(F32), latent_halo_ref, latent_ref, halo_ref, pay_ref, saved, wsum_ref,
+        (lhs_ref, weight_ref, radius_t_ref, hot_t_ref), consts, outs, scratch, keep,
+    )
+
+
+def back_kernel(width, next_d_own_ref, next_d_far_ref, next_grad_ref, halo_ref, pay_ref, *refs):
+    lhs_ref, weight_ref, radius_t_ref, hot_t_ref, wsum_ref = refs[:5]
+    saved = tuple(ref[...] for ref in refs[5:11])
+    w = Step(refs[11:19], 0)
+    outs = refs[19:23]
+    scratch = refs[23:]
     d_both = jnp.concatenate([next_d_own_ref[...], next_d_far_ref[...]], axis=1).astype(BF)
-    grad_in_ref[...] = dot_tn(next_latent_ref[...], d_both)
-    d_new = next_grad_ref[...] + dot_nt(d_both, next_in_ref[...])
-    fill_pre(halo_ref[:, :L], halo_ref[:, L:], own_ref[...], pay_ref[:, L:], edge_geo_ref[...], far_ref, near_ref)
-    shifts, g2, bias2 = edge_constants(edge_geo_ref, mid_w_ref, biases_ref, mid2_ref, mid2_t_ref)
-    occ = column(pay_ref[:, L:], 2)
-    saved = (
-        sums_low_ref[...], message_ref[...], half_ref[...], first_low_ref[...], normed_ref[...], inv_ref[...],
-    )
-    d_sums, d_latent, grad_out, grad_first, grad_second, small = node_backward(
-        d_new, latent_ref[...], occ, wsum_ref[...], saved, out_w_ref[...], first_w_ref[...], second_w_ref[...],
-        gain_ref[...],
-    )
-    sums_ref[...] = d_sums
-    grad_ref[...] = d_new + d_latent
-    store_node_grads(grads_ref, small_ref, grad_out, grad_first, grad_second, small)
-    edges_backward(
-        width, lhs_ref, weight_ref, radius_t_ref, hot_t_ref, far_ref, near_ref, shifts, g2, mid2_ref, mid2_t_ref, bias2,
-        sums_ref, d_own_ref, d_far_ref, mid_ref, rows_ref, bias_ref,
-    )
-    geo = geo_grads(rows_ref[...], d_far_ref[...], halo_ref[:, L:], d_own_ref[...], pay_ref[:, L:])
-    store_edge_grads(grads_ref, small_ref, mid_ref[...], bias_ref[...], geo)
-
-
-def last_kernel(d_own_ref, d_far_ref, grad_ref, latent_ref, edge_in_ref, pay_ref, out_ref, grad_in_ref):
+    d_new = next_grad_ref[...] + dot_nt(d_both, refs[11][1])
+    consts = prepare(
+        w, halo_ref[:, :L], halo_ref[:, L:], pay_ref[:, :L], pay_ref[:, L:], *scratch[:2], *scratch[6:8]
+    )
+    backward(
+        width, w, d_new, halo_ref, pay_ref, halo_ref, pay_ref, saved, wsum_ref,
+        (lhs_ref, weight_ref, radius_t_ref, hot_t_ref), consts, outs, scratch, None,
+    )
+
+
+def last_kernel(d_own_ref, d_far_ref, grad_ref, edge_in_ref, pay_ref, out_ref):
     d_both = jnp.concatenate([d_own_ref[...], d_far_ref[...]], axis=1).astype(BF)
-    grad_in_ref[...] = dot_tn(latent_ref[...], d_both)
-    occ = column(pay_ref[:, L:], 2)
-    out_ref[...] = occ * (grad_ref[...] + dot_nt(d_both, edge_in_ref[...]))
-
-
-def call(kernel, outs, scratch, *args):
+    out_ref[...] = column(pay_ref[:, L:], 2) * (grad_ref[...] + dot_nt(d_both, edge_in_ref[0]))
+
+
+def unpack_kernel(scale, rows_ref, in_ref, geo_ref, mid_ref, out_ref, first_ref, second_ref, bias_ref, gain_ref):
+    gains = []
+    for t in range(STEPS):
+        def take(start, size, base=t * GROWS):
+            return rows_ref[base + start : base + start + size, :].astype(F32) * scale
+
+        in_ref[t, :, :L] = take(0, L)
+        in_ref[t, :, L:] = take(L, L)
+        mid_ref[t] = take(2 * L, L)
+        out_ref[t] = take(3 * L, L)
+        first_ref[t] = take(4 * L, 2 * L)
+        second_ref[t] = take(6 * L, L)
+        small = take(7 * L, 16)
+        bias_ref[t] = small[:5]
+        geo_ref[t] = small[6:9]
+        gains.append(small[5:6])
+    gain_ref[...] = jnp.concatenate(gains, axis=0)
+
+
+def call(kernel, outs, scratch, *args, mib=8):
     return pl.pallas_call(
         kernel,
         out_shape=[jax.ShapeDtypeStruct(shape, dtype) for shape, dtype in outs],
         in_specs=[pl.BlockSpec(memory_space=pltpu.VMEM)] * len(args),
         out_specs=[pl.BlockSpec(memory_space=pltpu.VMEM)] * len(outs),
         scratch_shapes=[pltpu.VMEM(shape, dtype) for shape, dtype in scratch],
-        compiler_params=pltpu.CompilerParams(vmem_limit_bytes=48 * 1024 * 1024),
+        compiler_params=pltpu.CompilerParams(vmem_limit_bytes=mib * 1024 * 1024),
     )(*args)
 
 
@@ -470,10 +508,10 @@
 def total_over_devices(rows):
     axes = ("gx", "gy")
     count = lax.axis_size("gx") * lax.axis_size("gy")
-    parts = lax.all_to_all(rows.astype(BF).reshape(count, -1, L), axes, 0, 0)
+    parts = lax.all_to_all(rows.reshape(count, -1, L), axes, 0, 0)
     mine = jnp.sum(parts.astype(F32), axis=0).astype(BF)
     spread = jnp.broadcast_to(mine[None], (count,) + mine.shape)
-    return lax.all_to_all(spread, axes, 0, 0).reshape(-1, L).astype(F32)
+    return lax.all_to_all(spread, axes, 0, 0).reshape(-1, L)
 
 
 def on_device(
@@ -507,69 +545,57 @@
     section = jnp.stack(sections)
     final = [section[:, 1], from_behind(section[:, 2], "gx", 1), from_behind(section[:, 0], "gx", -1)]
     arrived = jnp.concatenate([piece.reshape(-1, 2 * L) for piece in final], axis=0)
-    v0, own0, pay = call(
-        place_kernel, [((slots, L), BF), ((slots, L), F32), ((slots, 2 * L), BF)], [], arrived, edge_in[0]
-    )
+    (pay,) = call(place_kernel, [((slots, 2 * L), BF)], [], arrived)
     halo = with_halo(pay.reshape(cells_x, cells_y, cap_size, 2 * L)).reshape(halo_rows, 2 * L)
-
-    def weights(t):
-        return (edge_geo[t], edge_mid[t], edge_out[t], node_in[t], node_out[t], biases[t], ln_gain[t][None, :])
-
+    weights = (edge_in, edge_geo, edge_mid, edge_out, node_in, node_out, biases, ln_gain)
     node = ((slots, L), F32)
     node_low = ((slots, L), BF)
     geometry = [((EDGES, 2 * L), BF), ((EDGES, L), BF), ((L, EDGES), F32), ((L, EDGES), F32), ((80, EDGES), BF)]
+    wide = ((2 * L, 2 * L), BF)
     edge_scratch = [((halo_rows, L), F32), node, node]
-    sums_scratch = [((2 * L, 2 * L), F32), ((96, 2 * L), F32), ((8, 2 * L), F32)]
-    sums_scratch += [((2 * L, 2 * L), BF)] * 2 + [((8, L), F32)]
     firsts = call(
         functools.partial(first_kernel, width),
-        geometry + [node_low, node, node_low, node, node_low, node_low, node, node_low, node, node],
-        edge_scratch + [((2 * L, 2 * L), BF)],
-        halo, pay, own0, v0, *weights(0), edge_in[1],
-    )
-    lhs, weight, weight_t, radius_t, hot_t = firsts[:5]
-    v1, own1, far1 = firsts[5:8]
-    saved0 = firsts[8:]
-    far1_halo = with_halo(far1.reshape(cells_x, cells_y, cap_size, L)).reshape(halo_rows, L)
-    edge_outs = [node, ((halo_rows, L), F32), node, ((768, L), F32)]
+        geometry + [node_low, node, node_low, node_low, node, node_low, node, node],
+        edge_scratch + [wide],
+        halo, pay, *weights,
+        mib=20,
+    )
+    lhs, weight, weight_t, radius_t, hot_t, v1, wsum0 = firsts[:7]
+    saved0 = firsts[7:]
+    v1_halo = with_halo(v1.reshape(cells_x, cells_y, cap_size, L)).reshape(halo_rows, L)
+    edge_outs = [node, ((halo_rows, L), F32), node, ((GROWS, L), BF)]
+    edge_scratch += [((2 * L, 2 * L), F32), ((96, 2 * L), F32), ((8, 2 * L), F32), wide, wide, ((8, L), F32)]
+    kept = ((slots // (2 * CAP) * EDGES, 2 * L), BF)
     v2, d_own1, d_far1, grad1, grads1 = call(
         functools.partial(middle_kernel, width),
         [node_low] + edge_outs,
-        edge_scratch + [node] + sums_scratch,
-        far1_halo, halo, pay, own1, v1, cotangent.reshape(slots, L), lhs, weight, weight_t, radius_t, hot_t, *weights(1),
+        edge_scratch + [node, kept, kept, kept],
+        v1_halo, halo, pay, v1, cotangent.reshape(slots, L), lhs, weight, weight_t, radius_t, hot_t, *weights,
+        mib=44,
     )
     d_far1 = fold_halo(d_far1.reshape(cells_x + 2, width, cap_size, L)).reshape(slots, L)
-    d_own0, d_far0, grad0, grads0, grad_in1 = call(
+    d_own0, d_far0, grad0, grads0 = call(
         functools.partial(back_kernel, width),
-        edge_outs + [((L, 2 * L), F32)],
-        edge_scratch + sums_scratch,
-        d_own1, d_far1, grad1, v1, edge_in[1], halo, pay, own0, v0, lhs, weight, radius_t, hot_t, *saved0, *weights(0),
+        edge_outs,
+        edge_scratch,
+        d_own1, d_far1, grad1, halo, pay, lhs, weight, radius_t, hot_t, wsum0, *saved0, *weights,
+        mib=20,
     )
     d_far0 = fold_halo(d_far0.reshape(cells_x + 2, width, cap_size, L)).reshape(slots, L)
-    latent_grad, grad_in0 = call(
-        last_kernel, [node, ((L, 2 * L), F32)], [], d_own0, d_far0, grad0, v0, edge_in[0], pay
-    )
-    packed = jnp.concatenate(
+    (latent_grad,) = call(last_kernel, [node], [], d_own0, d_far0, grad0, edge_in, pay)
+    total = total_over_devices(jnp.concatenate([grads0, grads1], axis=0))
+    scale = float(slots * count_x * count_y) ** -0.5
+    grads = call(
+        functools.partial(unpack_kernel, scale),
         [
-            grad_in0[:, :L], grad_in0[:, L:], grads0, grad_in1[:, :L], grad_in1[:, L:], grads1,
+            ((STEPS, L, 2 * L), F32), ((STEPS, 3, L), F32), ((STEPS, L, L), F32), ((STEPS, L, L), F32),
+            ((STEPS, 2 * L, L), F32), ((STEPS, L, L), F32), ((STEPS, 5, L), F32), ((STEPS, L), F32),
         ],
-        axis=0,
-    )
-    total = total_over_devices(packed) * (float(slots * count_x * count_y) ** -0.5)
-    total = total.reshape(STEPS, GROWS, L)
+        [],
+        total,
+    )
     cells = (cells_x, cells_y, cap_size, width_l)
-    return (
-        v2.reshape(cells),
-        latent_grad.reshape(cells),
-        jnp.concatenate([total[:, :L], total[:, L : 2 * L]], axis=2),
-        total[:, 902:905],
-        total[:, 2 * L : 3 * L],
-        total[:, 3 * L : 4 * L],
-        total[:, 4 * L : 6 * L],
-        total[:, 6 * L : 7 * L],
-        total[:, 896:901],
-        total[:, 901],
-    )
+    return (v2.reshape(cells), latent_grad.reshape(cells), *grads)
 
 
 def solution(mesh):

time: 202 us -> 156 us (0.77)
  blocking collectives: 41.3 us -> 0 us
  Pallas kernels: 101 us -> 64.8 us
  waiting for transfers between devices: 16.4 us -> 39.6 us
  starting transfers between devices: 32.9 us -> 42.7 us
  local copies, waits for them, and re-layouts: 8.22 us -> 5.83 us
    all_to_all x2 -> x0, blocking collectives: 41.3 us -> none  [the longest x1 23 us: total_over_devices(): parts = lax.all_to_all(rows.astype(BF).reshape(count, -1, L), axes, 0, 0)]
    pallas_call x6 -> x7, Pallas kernels: 101 us -> 64.8 us  [call(): pl.pallas_call(kernel, out_shape=[jax.ShapeDtypeStruct(shape, dtype) for...]
    all_to_all x0 -> x2, waiting for transfers between devices: none -> 15.6 us  [the longest x1 13.5 us: total_over_devices(): parts = lax.all_to_all(rows.reshape(count, -1, L), axes, 0, 0)]
    all_to_all x0 -> x2, starting transfers between devices: none -> 11.6 us  [the longest x1 8.49 us: total_over_devices(): parts = lax.all_to_all(rows.reshape(count, -1, L), axes, 0, 0)]
    ppermute x20, waiting for transfers between devices: 16.4 us -> 24.1 us  [from_behind(): lax.ppermute(value, axis, [(source, (source + steps) % count) for source...]
    slice x8 -> x0, local copies, waits for them, and re-layouts: 2.06 us -> none  [the longest x1 0.75 us: on_device(): total[:, 6 * L:7 * L]]
    unnamed x36 -> x30, local copies, waits for them, and re-layouts: 5.83 us -> 4.74 us
  transfers between devices with their start and end apart: 20 -> 22, of which waited for: 14 -> 15; matrix products, arithmetic and copies ran while one was open for 0% -> 1% of each run, Pallas kernels for 0% -> 1%
where the time goes in v1:
time: 156 us; the launch traced here: 155 us
  Pallas kernels  64.8 us (42%)
  starting transfers between devices  42.7 us (27%)
  waiting for transfers between devices  39.6 us (25%)
  local copies, waits for them, and re-layouts  5.83 us (4%)
    pallas_call x7, Pallas kernels, call(): pl.pallas_call(kernel, out_shape=[jax.ShapeDtypeStruct(shape, dtype) for...  64.8 us
    ppermute x20, starting transfers between devices, from_behind(): lax.ppermute(value, axis, [(source, (source + steps) % count) for source...  31.1 us
    ppermute x20, waiting for transfers between devices, from_behind(): lax.ppermute(value, axis, [(source, (source + steps) % count) for source...  24.1 us
    all_to_all x1, waiting for transfers between devices, total_over_devices(): parts = lax.all_to_all(rows.reshape(count, -1, L), axes, 0, 0)  13.5 us
    all_to_all x1, starting transfers between devices, total_over_devices(): parts = lax.all_to_all(rows.reshape(count, -1, L), axes, 0, 0)  8.49 us
    unnamed x30, local copies, waits for them, and re-layouts  4.74 us
    all_to_all x1, starting transfers between devices, total_over_devices(): return lax.all_to_all(spread, axes, 0, 0).reshape(-1, L)  3.15 us
  transfers between devices with their start and end apart: 22, of which 15 were waited for; matrix products, arithmetic and copies ran while one was open for 1% of the time, Pallas kernels for 1%

profile of v1, /device:TPU:1, one launch (start us, length us, event | category | flops | bytes accessed | tf_op | source)
XLA Modules:
  0.0 155.5 jit_solution(14970694148050715041)
XLA Ops:
  0.7 0.7 copy-done.8
  1.3 0.7 copy-done.10
  2.0 0.7 copy-done.11
  2.8 0.9 copy-done.6
  3.7 0.6 shard_map.204
  4.3 2.2 %collective-permute-start = (bf16[3,48,256]{2,1,0:T(8,128)(2,1)S(1)}, bf16[3,48,256]{2,1,0:T(8,128)(2,1)S(1)}, u32[]{:S(2)}, u32[]{:S(2)}) collective-permute-start(bf16[3,48,256]{2,1,0:T(8,128)(2,1)S(1)} %get-tuple-element.96), channel_id=1, source_target_pairs={{0,1},{1,2},{2,3},{3,0},{4,5},{5,6},{6,7},{7,4},{8,9},{9,10},{10,1... | collective-permute-start | bytes 221192 | tf_op jit(solution)/shard_map/ppermute | solution.py:484
  6.5 2.1 %collective-permute-start.1 = (bf16[3,48,256]{2,1,0:T(8,128)(2,1)S(1)}, bf16[3,48,256]{2,1,0:T(8,128)(2,1)S(1)}, u32[]{:S(2)}, u32[]{:S(2)}) collective-permute-start(bf16[3,48,256]{2,1,0:T(8,128)(2,1)S(1)} %get-tuple-element.97), channel_id=1, source_target_pairs={{0,3},{1,0},{2,1},{3,2},{4,7},{5,4},{6,5},{7,6},{8,11},{9,8},{10,9... | collective-permute-start | bytes 221192 | tf_op jit(solution)/shard_map/ppermute | solution.py:484
  8.5 1.8 %collective-permute-done = bf16[3,48,256]{2,1,0:T(8,128)(2,1)S(1)} collective-permute-done((bf16[3,48,256]{2,1,0:T(8,128)(2,1)S(1)}, bf16[3,48,256]{2,1,0:T(8,128)(2,1)S(1)}, u32[]{:S(2)}, u32[]{:S(2)}) %collective-permute-start) | collective-permute-done | bytes 73760 | tf_op jit(solution)/shard_map/ppermute | solution.py:484
  10.3 1.3 collective-permute-done.1
  11.7 1.1 collective-permute-start.3
  12.8 1.2 collective-permute-start.2
  14.0 2.0 %collective-permute-done.3 = bf16[3,48,256]{2,1,0:T(8,128)(2,1)S(1)} collective-permute-done((bf16[3,48,256]{2,1,0:T(8,128)(2,1)S(1)}, bf16[3,48,256]{2,1,0:T(8,128)(2,1)S(1)}, u32[]{:S(2)}, u32[]{:S(2)}) %collective-permute-start.3) | collective-permute-done | bytes 73760 | tf_op jit(solution)/shard_map/ppermute | solution.py:484
  16.4 2.5 %collective-permute-start.4 = (bf16[1,8,8,256]{3,2,1,0:T(8,128)(2,1)S(1)}, bf16[1,8,8,256]{3,2,1,0:T(8,128)(2,1)S(1)}, u32[]{:S(2)}, u32[]{:S(2)}) collective-permute-start(bf16[1,8,8,256]{3,2,1,0:T(8,128)(2,1)S(1)} %get-tuple-element.90), channel_id=1, source_target_pairs={{0,4},{4,8},{8,12},{12,16},{16,20},{20,24},{24,28},{28,0},{1,5},{5... | collective-permute-start | bytes 98312 | tf_op jit(solution)/shard_map/ppermute | solution.py:484
  19.2 0.7 collective-permute-done.4
  19.9 2.3 %collective-permute-done.5 = bf16[1,8,8,256]{3,2,1,0:T(8,128)(2,1)S(1)} collective-permute-done((bf16[1,8,8,256]{3,2,1,0:T(8,128)(2,1)S(1)}, bf16[1,8,8,256]{3,2,1,0:T(8,128)(2,1)S(1)}, u32[]{:S(2)}, u32[]{:S(2)}) %collective-permute-start.5) | collective-permute-done | bytes 32800 | tf_op jit(solution)/shard_map/ppermute | solution.py:484
  22.7 2.9 %collective-permute-start.7 = (bf16[10,1,8,256]{3,2,1,0:T(8,128)(2,1)S(1)}, bf16[10,1,8,256]{3,2,1,0:T(8,128)(2,1)S(1)}, u32[]{:S(2)}, u32[]{:S(2)}) collective-permute-start(bf16[10,1,8,256]{3,2,1,0:T(8,128)(2,1)S(1)} %get-tuple-element.89), channel_id=1, source_target_pairs={{0,3},{1,0},{2,1},{3,2},{4,7},{5,4},{6,5},{7,6},{8,11},{9,8},{10,9... | collective-permute-start | bytes 122888 | tf_op jit(solution)/shard_map/ppermute | solution.py:484
  25.7 1.4 collective-permute-done.6
  27.2 0.6 copy-done.7
  27.8 13.5 %shard_map.206 = (bf16[576,256]{1,0:T(8,128)(2,1)S(1)}, bf16[576,128]{1,0:T(8,128)(2,1)S(1)}, f32[128,576]{1,0:T(8,128)S(1)}, f32[128,576]{1,0:T(8,128)S(1)}, bf...) custom-call(bf16[800,256]{1,0:T(8,128)(2,1)S(1)} %bitcast.64, ...), custom_call_target="tpu_custom_call" | custom-call | tf_op jit(solution)/shard_map/pallas_call | solution.py:472
  41.3 1.2 collective-permute-start.8
  42.5 1.6 %collective-permute-start.9 = (bf16[1,8,8,128]{3,2,1,0:T(8,128)(2,1)S(1)}, bf16[1,8,8,128]{3,2,1,0:T(8,128)(2,1)S(1)}, u32[]{:S(2)}, u32[]{:S(2)}) collective-permute-start(bf16[1,8,8,128]{3,2,1,0:T(8,128)(2,1)S(1)} %get-tuple-element.109), channel_id=1, source_target_pairs={{0,28},{4,0},{8,4},{12,8},{16,12},{20,16},{24,20},{28,24},{1,29},{... | collective-permute-start | bytes 49160 | tf_op jit(solution)/shard_map/ppermute | solution.py:484
  44.1 0.6 collective-permute-done.8
  44.7 1.0 collective-permute-done.9
  46.3 3.2 %collective-permute-start.11 = (bf16[10,1,8,128]{3,2,1,0:T(8,128)(2,1)S(1)}, bf16[10,1,8,128]{3,2,1,0:T(8,128)(2,1)S(1)}, u32[]{:S(2)}, u32[]{:S(2)}) collective-permute-start(bf16[10,1,8,128]{3,2,1,0:T(8,128)(2,1)S(1)} %get-tuple-element.107), channel_id=1, source_target_pairs={{0,3},{1,0},{2,1},{3,2},{4,7},{5,4},{6,5},{7,6},{8,11},{9,8},{10,9... | collective-permute-start | bytes 61448 | tf_op jit(solution)/shard_map/ppermute | solution.py:484
  49.4 1.1 collective-permute-done.10
  50.6 27.3 %shard_map.207 = (bf16[512,128]{1,0:T(8,128)(2,1)}, f32[512,128]{1,0:T(8,128)S(1)}, f32[800,128]{1,0:T(8,128)S(1)}, f32[512,128]{1,0:T(8,128)S(1)}, bf16[1024,128]{1,0:T(8,128)(2,1)S(1)}) custom-call(bf16[800,128]{1,0:T(8,128)(2,1)S(1)} %bitcast.73, bf16[800,256]{1,0:T(8,128)(2,1)S(1)} %bitcast.65, bf16[512,256]{1,0:T(8,128)(2,1)S(1)} %shard_map.205.pay_ref, ...), custom_call_target="tpu_custom_call" | custom-call | tf_op jit(solution)/shard_map/pallas_call | solution.py:472
  77.9 1.4 collective-permute-start.12
  79.4 1.9 %collective-permute-start.13 = (bf16[1,10,8,128]{3,2,1,0:T(8,128)(2,1)S(1)}, bf16[1,10,8,128]{3,2,1,0:T(8,128)(2,1)S(1)}, u32[]{:S(2)}, u32[]{:S(2)}) collective-permute-start(bf16[1,10,8,128]{3,2,1,0:T(8,128)(2,1)S(1)} %get-tuple-element.101), channel_id=1, source_target_pairs={{0,28},{4,0},{8,4},{12,8},{16,12},{20,16},{24,20},{28,24},{1,29},{... | collective-permute-start | bytes 61448 | tf_op jit(solution)/shard_map/ppermute | solution.py:484
  81.3 0.6 collective-permute-done.12
  81.9 1.2 collective-permute-done.13
  83.1 0.6 collective-permute-start.14
  83.7 3.0 %collective-permute-start.15 = (bf16[8,1,8,128]{3,2,1,0:T(8,128)(2,1)S(1)}, bf16[8,1,8,128]{3,2,1,0:T(8,128)(2,1)S(1)}, u32[]{:S(2)}, u32[]{:S(2)}) collective-permute-start(bf16[8,1,8,128]{3,2,1,0:T(8,128)(2,1)S(1)} %get-tuple-element.105), channel_id=1, source_target_pairs={{0,3},{1,0},{2,1},{3,2},{4,7},{5,4},{6,5},{7,6},{8,11},{9,8},{10,9... | collective-permute-start | bytes 49160 | tf_op jit(solution)/shard_map/ppermute | solution.py:484
  86.8 0.8 collective-permute-done.14
  87.6 21.2 %shard_map.208 = (f32[512,128]{1,0:T(8,128)S(1)}, f32[800,128]{1,0:T(8,128)S(1)}, f32[512,128]{1,0:T(8,128)S(1)}, bf16[1024,128]{1,0:T(8,128)(2,1)S(1)}) custom-call(f32[512,128]{1,0:T(8,128)S(1)} %get-tuple-element.47.next_d_own_ref, f32[512,128]{1,0:T(8,128)S(1)} %bitcast.70, f32[512,128]{1,0:T(8,128)S(1)} %get-tuple-element.49.next_grad_ref, ...), custom_call_target="tpu_custom_call" | custom-call | tf_op jit(solution)/shard_map/pallas_call | solution.py:472
  108.8 0.8 pad_maximum_fusion
  109.6 8.5 %all-to-all-start = ((bf16[32,64,128]{2,1,0:T(8,128)(2,1)}), bf16[32,64,128]{2,1,0:T(8,128)(2,1)S(1)}, u32[]{:S(2)}, u32[]{:S(2)}) async-start(bf16[32,64,128]{2,1,0:T(8,128)(2,1)} %bitcast.37), calls=%async_computation | async-start | bytes 1048576 | tf_op jit(solution)/shard_map/all_to_all | solution.py:511
  118.2 1.7 %collective-permute-start.16 = (bf16[1,10,8,128]{3,2,1,0:T(8,128)(2,1)S(1)}, bf16[1,10,8,128]{3,2,1,0:T(8,128)(2,1)S(1)}, u32[]{:S(2)}, u32[]{:S(2)}) collective-permute-start(bf16[1,10,8,128]{3,2,1,0:T(8,128)(2,1)S(1)} %get-tuple-element.98), channel_id=1, source_target_pairs={{0,4},{4,8},{8,12},{12,16},{16,20},{20,24},{24,28},{28,0},{1,5},{5... | collective-permute-start | bytes 61448 | tf_op jit(solution)/shard_map/ppermute | solution.py:484
  119.9 13.5 %all-to-all-done = bf16[32,64,128]{2,1,0:T(8,128)(2,1)S(1)} async-done(((bf16[32,64,128]{2,1,0:T(8,128)(2,1)}), bf16[32,64,128]{2,1,0:T(8,128)(2,1)S(1)}, u32[]{:S(2)}, u32[]{:S(2)}) %all-to-all-start) | async-done | bytes 524320 | tf_op jit(solution)/shard_map/all_to_all | solution.py:511
  133.5 0.9 broadcast_in_dim.10
  134.4 3.2 %all-to-all-start.1 = ((bf16[32,64,128]{2,1,0:T(8,128)(2,1)}), bf16[32,64,128]{2,1,0:T(8,128)(2,1)S(1)}, u32[]{:S(2)}, u32[]{:S(2)}) async-start(bf16[32,64,128]{2,1,0:T(8,128)(2,1)} %broadcast_in_dim.10), calls=%async_computation.1 | async-start | bytes 1048576 | tf_op jit(solution)/shard_map/all_to_all | solution.py:514
  137.6 1.4 collective-permute-start.18
  139.1 1.9 %collective-permute-start.19 = (bf16[8,1,8,128]{3,2,1,0:T(8,128)(2,1)S(1)}, bf16[8,1,8,128]{3,2,1,0:T(8,128)(2,1)S(1)}, u32[]{:S(2)}, u32[]{:S(2)}) collective-permute-start(bf16[8,1,8,128]{3,2,1,0:T(8,128)(2,1)S(1)} %get-tuple-element.103), channel_id=1, source_target_pairs={{0,3},{1,0},{2,1},{3,2},{4,7},{5,4},{6,5},{7,6},{8,11},{9,8},{10,9... | collective-permute-start | bytes 49160 | tf_op jit(solution)/shard_map/ppermute | solution.py:484
  141.0 9.3 %collective-permute-done.18 = bf16[8,1,8,128]{3,2,1,0:T(8,128)(2,1)S(1)} collective-permute-done((bf16[8,1,8,128]{3,2,1,0:T(8,128)(2,1)S(1)}, bf16[8,1,8,128]{3,2,1,0:T(8,128)(2,1)S(1)}, u32[]{:S(2)}, u32[]{:S(2)}) %collective-permute-start.18) | collective-permute-done | bytes 16416 | tf_op jit(solution)/shard_map/ppermute | solution.py:484
  150.4 0.9 shard_map.209
  151.3 2.0 %all-to-all-done.1 = bf16[32,64,128]{2,1,0:T(8,128)(2,1)S(1)} async-done(((bf16[32,64,128]{2,1,0:T(8,128)(2,1)}), bf16[32,64,128]{2,1,0:T(8,128)(2,1)S(1)}, u32[]{:S(2)}, u32[]{:S(2)}) %all-to-all-start.1) | async-done | bytes 524320 | tf_op jit(solution)/shard_map/all_to_all | solution.py:514
  153.3 0.9 shard_map.210
  154.3 0.6 copy.32
  154.9 0.6 copy.33
  (73 shorter events, 2.5 us)
Async XLA Ops:
  0.6 0.7 copy-start.8
  1.3 0.7 copy-start.10
  2.0 0.7 copy-start.11
  2.8 0.9 copy-start.6
  4.3 6.0 %collective-permute-start = (bf16[3,48,256]{2,1,0:T(8,128)(2,1)S(1)}, bf16[3,48,256]{2,1,0:T(8,128)(2,1)S(1)}, u32[]{:S(2)}, u32[]{:S(2)}) collective-permute-start(bf16[3,48,256]{2,1,0:T(8,128)(2,1)S(1)} %get-tuple-element.96), channel_id=1, source_target_pairs={{0,1},{1,2},{2,3},{3,0},{4,5},{5,6},{6,7},{7,4},{8,9},{9,10},{10,1... | collective-permute-start | bytes 221192 | tf_op jit(solution)/shard_map/ppermute | solution.py:484
  6.5 5.2 %collective-permute-start.1 = (bf16[3,48,256]{2,1,0:T(8,128)(2,1)S(1)}, bf16[3,48,256]{2,1,0:T(8,128)(2,1)S(1)}, u32[]{:S(2)}, u32[]{:S(2)}) collective-permute-start(bf16[3,48,256]{2,1,0:T(8,128)(2,1)S(1)} %get-tuple-element.97), channel_id=1, source_target_pairs={{0,3},{1,0},{2,1},{3,2},{4,7},{5,4},{6,5},{7,6},{8,11},{9,8},{10,9... | collective-permute-start | bytes 221192 | tf_op jit(solution)/shard_map/ppermute | solution.py:484
  11.7 4.2 %collective-permute-start.3 = (bf16[3,48,256]{2,1,0:T(8,128)(2,1)S(1)}, bf16[3,48,256]{2,1,0:T(8,128)(2,1)S(1)}, u32[]{:S(2)}, u32[]{:S(2)}) collective-permute-start(bf16[3,48,256]{2,1,0:T(8,128)(2,1)S(1)} %get-tuple-element.93), channel_id=1, source_target_pairs={{0,28},{4,0},{8,4},{12,8},{16,12},{20,16},{24,20},{28,24},{1,29},{... | collective-permute-start | bytes 221192 | tf_op jit(solution)/shard_map/ppermute | solution.py:484
  12.8 3.1 %collective-permute-start.2 = (bf16[3,48,256]{2,1,0:T(8,128)(2,1)S(1)}, bf16[3,48,256]{2,1,0:T(8,128)(2,1)S(1)}, u32[]{:S(2)}, u32[]{:S(2)}) collective-permute-start(bf16[3,48,256]{2,1,0:T(8,128)(2,1)S(1)} %get-tuple-element.94), channel_id=1, source_target_pairs={{0,4},{4,8},{8,12},{12,16},{16,20},{20,24},{24,28},{28,0},{1,5},{5... | collective-permute-start | bytes 221192 | tf_op jit(solution)/shard_map/ppermute | solution.py:484
  16.4 3.5 %collective-permute-start.4 = (bf16[1,8,8,256]{3,2,1,0:T(8,128)(2,1)S(1)}, bf16[1,8,8,256]{3,2,1,0:T(8,128)(2,1)S(1)}, u32[]{:S(2)}, u32[]{:S(2)}) collective-permute-start(bf16[1,8,8,256]{3,2,1,0:T(8,128)(2,1)S(1)} %get-tuple-element.90), channel_id=1, source_target_pairs={{0,4},{4,8},{8,12},{12,16},{16,20},{20,24},{24,28},{28,0},{1,5},{5... | collective-permute-start | bytes 98312 | tf_op jit(solution)/shard_map/ppermute | solution.py:484
  18.9 3.3 %collective-permute-start.5 = (bf16[1,8,8,256]{3,2,1,0:T(8,128)(2,1)S(1)}, bf16[1,8,8,256]{3,2,1,0:T(8,128)(2,1)S(1)}, u32[]{:S(2)}, u32[]{:S(2)}) collective-permute-start(bf16[1,8,8,256]{3,2,1,0:T(8,128)(2,1)S(1)} %get-tuple-element.91), channel_id=1, source_target_pairs={{0,28},{4,0},{8,4},{12,8},{16,12},{20,16},{24,20},{28,24},{1,29},{... | collective-permute-start | bytes 98312 | tf_op jit(solution)/shard_map/ppermute | solution.py:484
  22.3 3.3 %copy-start.12 = (bf16[2,3,128]{2,0,1:T(2,128)(2,1)S(1)}, bf16[2,3,128]{2,0,1:T(2,128)(2,1)}, u32[]{:S(2)}) copy-start(bf16[2,3,128]{2,0,1:T(2,128)(2,1)} %param.19) | copy-start | bytes 4612
  22.3 3.3 %copy-start.9 = (bf16[2,5,128]{2,0,1:T(2,128)(2,1)S(1)}, bf16[2,5,128]{2,0,1:T(2,128)(2,1)}, u32[]{:S(2)}) copy-start(bf16[2,5,128]{2,0,1:T(2,128)(2,1)} %param.24) | copy-start | bytes 7684
  22.3 4.8 %collective-permute-start.6 = (bf16[10,1,8,256]{3,2,1,0:T(8,128)(2,1)S(1)}, bf16[10,1,8,256]{3,2,1,0:T(8,128)(2,1)S(1)}, u32[]{:S(2)}, u32[]{:S(2)}) collective-permute-start(bf16[10,1,8,256]{3,2,1,0:T(8,128)(2,1)S(1)} %get-tuple-element.88), channel_id=1, source_target_pairs={{0,1},{1,2},{2,3},{3,0},{4,5},{5,6},{6,7},{7,4},{8,9},{9,10},{10,1... | collective-permute-start | bytes 122888 | tf_op jit(solution)/shard_map/ppermute | solution.py:484
  22.7 4.4 %collective-permute-start.7 = (bf16[10,1,8,256]{3,2,1,0:T(8,128)(2,1)S(1)}, bf16[10,1,8,256]{3,2,1,0:T(8,128)(2,1)S(1)}, u32[]{:S(2)}, u32[]{:S(2)}) collective-permute-start(bf16[10,1,8,256]{3,2,1,0:T(8,128)(2,1)S(1)} %get-tuple-element.89), channel_id=1, source_target_pairs={{0,3},{1,0},{2,1},{3,2},{4,7},{5,4},{6,5},{7,6},{8,11},{9,8},{10,9... | collective-permute-start | bytes 122888 | tf_op jit(solution)/shard_map/ppermute | solution.py:484
  25.6 1.6 %copy-start = (bf16[2,128,256]{2,1,0:T(8,128)(2,1)S(1)}, bf16[2,128,256]{2,1,0:T(8,128)(2,1)}, u32[]{:S(2)}) copy-start(bf16[2,128,256]{2,1,0:T(8,128)(2,1)} %edge_in_ref.1) | copy-start | bytes 393220
  25.6 1.6 %copy-start.1 = (bf16[2,256,128]{2,1,0:T(8,128)(2,1)S(1)}, bf16[2,256,128]{2,1,0:T(8,128)(2,1)}, u32[]{:S(2)}) copy-start(bf16[2,256,128]{2,1,0:T(8,128)(2,1)} %refs_15_.1) | copy-start | bytes 393220
  25.7 1.6 %copy-start.2 = (bf16[2,128,128]{2,1,0:T(8,128)(2,1)S(1)}, bf16[2,128,128]{2,1,0:T(8,128)(2,1)}, u32[]{:S(2)}) copy-start(bf16[2,128,128]{2,1,0:T(8,128)(2,1)} %refs_13_.1) | copy-start | bytes 196612
  25.7 1.6 %copy-start.3 = (bf16[2,128,128]{2,1,0:T(8,128)(2,1)S(1)}, bf16[2,128,128]{2,1,0:T(8,128)(2,1)}, u32[]{:S(2)}) copy-start(bf16[2,128,128]{2,1,0:T(8,128)(2,1)} %refs_14_.1) | copy-start | bytes 196612
  25.7 1.6 copy-start.4
  27.2 0.7 copy-start.7
  41.3 3.4 %collective-permute-start.8 = (bf16[1,8,8,128]{3,2,1,0:T(8,128)(2,1)S(1)}, bf16[1,8,8,128]{3,2,1,0:T(8,128)(2,1)S(1)}, u32[]{:S(2)}, u32[]{:S(2)}) collective-permute-start(bf16[1,8,8,128]{3,2,1,0:T(8,128)(2,1)S(1)} %get-tuple-element.108), channel_id=1, source_target_pairs={{0,4},{4,8},{8,12},{12,16},{16,20},{20,24},{24,28},{28,0},{1,5},{5... | collective-permute-start | bytes 49160 | tf_op jit(solution)/shard_map/ppermute | solution.py:484
  42.5 3.2 %collective-permute-start.9 = (bf16[1,8,8,128]{3,2,1,0:T(8,128)(2,1)S(1)}, bf16[1,8,8,128]{3,2,1,0:T(8,128)(2,1)S(1)}, u32[]{:S(2)}, u32[]{:S(2)}) collective-permute-start(bf16[1,8,8,128]{3,2,1,0:T(8,128)(2,1)S(1)} %get-tuple-element.109), channel_id=1, source_target_pairs={{0,28},{4,0},{8,4},{12,8},{16,12},{20,16},{24,20},{28,24},{1,29},{... | collective-permute-start | bytes 49160 | tf_op jit(solution)/shard_map/ppermute | solution.py:484
  45.7 4.8 %collective-permute-start.10 = (bf16[10,1,8,128]{3,2,1,0:T(8,128)(2,1)S(1)}, bf16[10,1,8,128]{3,2,1,0:T(8,128)(2,1)S(1)}, u32[]{:S(2)}, u32[]{:S(2)}) collective-permute-start(bf16[10,1,8,128]{3,2,1,0:T(8,128)(2,1)S(1)} %get-tuple-element.106), channel_id=1, source_target_pairs={{0,1},{1,2},{2,3},{3,0},{4,5},{5,6},{6,7},{7,4},{8,9},{9,10},{10,1... | collective-permute-start | bytes 61448 | tf_op jit(solution)/shard_map/ppermute | solution.py:484
  46.3 4.3 %copy-start.5 = (bf16[8,8,8,128]{3,2,1,0:T(8,128)(2,1)S(1)}, bf16[8,8,8,128]{3,2,1,0:T(8,128)(2,1)}, u32[]{:S(2)}) copy-start(bf16[8,8,8,128]{3,2,1,0:T(8,128)(2,1)} %param.17) | copy-start | bytes 393220
  46.3 4.3 %collective-permute-start.11 = (bf16[10,1,8,128]{3,2,1,0:T(8,128)(2,1)S(1)}, bf16[10,1,8,128]{3,2,1,0:T(8,128)(2,1)S(1)}, u32[]{:S(2)}, u32[]{:S(2)}) collective-permute-start(bf16[10,1,8,128]{3,2,1,0:T(8,128)(2,1)S(1)} %get-tuple-element.107), channel_id=1, source_target_pairs={{0,3},{1,0},{2,1},{3,2},{4,7},{5,4},{6,5},{7,6},{8,11},{9,8},{10,9... | collective-permute-start | bytes 61448 | tf_op jit(solution)/shard_map/ppermute | solution.py:484
  77.9 4.0 %collective-permute-start.12 = (bf16[1,10,8,128]{3,2,1,0:T(8,128)(2,1)S(1)}, bf16[1,10,8,128]{3,2,1,0:T(8,128)(2,1)S(1)}, u32[]{:S(2)}, u32[]{:S(2)}) collective-permute-start(bf16[1,10,8,128]{3,2,1,0:T(8,128)(2,1)S(1)} %get-tuple-element.100), channel_id=1, source_target_pairs={{0,4},{4,8},{8,12},{12,16},{16,20},{20,24},{24,28},{28,0},{1,5},{5... | collective-permute-start | bytes 61448 | tf_op jit(solution)/shard_map/ppermute | solution.py:484
  79.4 3.7 %collective-permute-start.13 = (bf16[1,10,8,128]{3,2,1,0:T(8,128)(2,1)S(1)}, bf16[1,10,8,128]{3,2,1,0:T(8,128)(2,1)S(1)}, u32[]{:S(2)}, u32[]{:S(2)}) collective-permute-start(bf16[1,10,8,128]{3,2,1,0:T(8,128)(2,1)S(1)} %get-tuple-element.101), channel_id=1, source_target_pairs={{0,28},{4,0},{8,4},{12,8},{16,12},{20,16},{24,20},{28,24},{1,29},{... | collective-permute-start | bytes 61448 | tf_op jit(solution)/shard_map/ppermute | solution.py:484
  83.1 4.5 %collective-permute-start.14 = (bf16[8,1,8,128]{3,2,1,0:T(8,128)(2,1)S(1)}, bf16[8,1,8,128]{3,2,1,0:T(8,128)(2,1)S(1)}, u32[]{:S(2)}, u32[]{:S(2)}) collective-permute-start(bf16[8,1,8,128]{3,2,1,0:T(8,128)(2,1)S(1)} %get-tuple-element.104), channel_id=1, source_target_pairs={{0,1},{1,2},{2,3},{3,0},{4,5},{5,6},{6,7},{7,4},{8,9},{9,10},{10,1... | collective-permute-start | bytes 49160 | tf_op jit(solution)/shard_map/ppermute | solution.py:484
  83.7 3.9 %collective-permute-start.15 = (bf16[8,1,8,128]{3,2,1,0:T(8,128)(2,1)S(1)}, bf16[8,1,8,128]{3,2,1,0:T(8,128)(2,1)S(1)}, u32[]{:S(2)}, u32[]{:S(2)}) collective-permute-start(bf16[8,1,8,128]{3,2,1,0:T(8,128)(2,1)S(1)} %get-tuple-element.105), channel_id=1, source_target_pairs={{0,3},{1,0},{2,1},{3,2},{4,7},{5,4},{6,5},{7,6},{8,11},{9,8},{10,9... | collective-permute-start | bytes 49160 | tf_op jit(solution)/shard_map/ppermute | solution.py:484
  109.6 23.8 %all-to-all-start = ((bf16[32,64,128]{2,1,0:T(8,128)(2,1)}), bf16[32,64,128]{2,1,0:T(8,128)(2,1)S(1)}, u32[]{:S(2)}, u32[]{:S(2)}) async-start(bf16[32,64,128]{2,1,0:T(8,128)(2,1)} %bitcast.37), calls=%async_computation | async-start | bytes 1048576 | tf_op jit(solution)/shard_map/all_to_all | solution.py:511
  118.2 19.4 %collective-permute-start.16 = (bf16[1,10,8,128]{3,2,1,0:T(8,128)(2,1)S(1)}, bf16[1,10,8,128]{3,2,1,0:T(8,128)(2,1)S(1)}, u32[]{:S(2)}, u32[]{:S(2)}) collective-permute-start(bf16[1,10,8,128]{3,2,1,0:T(8,128)(2,1)S(1)} %get-tuple-element.98), channel_id=1, source_target_pairs={{0,4},{4,8},{8,12},{12,16},{16,20},{20,24},{24,28},{28,0},{1,5},{5... | collective-permute-start | bytes 61448 | tf_op jit(solution)/shard_map/ppermute | solution.py:484
  119.9 17.7 %collective-permute-start.17 = (bf16[1,10,8,128]{3,2,1,0:T(8,128)(2,1)S(1)}, bf16[1,10,8,128]{3,2,1,0:T(8,128)(2,1)S(1)}, u32[]{:S(2)}, u32[]{:S(2)}) collective-permute-start(bf16[1,10,8,128]{3,2,1,0:T(8,128)(2,1)S(1)} %get-tuple-element.99), channel_id=1, source_target_pairs={{0,28},{4,0},{8,4},{12,8},{16,12},{20,16},{24,20},{28,24},{1,29},{... | collective-permute-start | bytes 61448 | tf_op jit(solution)/shard_map/ppermute | solution.py:484
  134.4 19.0 %all-to-all-start.1 = ((bf16[32,64,128]{2,1,0:T(8,128)(2,1)}), bf16[32,64,128]{2,1,0:T(8,128)(2,1)S(1)}, u32[]{:S(2)}, u32[]{:S(2)}) async-start(bf16[32,64,128]{2,1,0:T(8,128)(2,1)} %broadcast_in_dim.10), calls=%async_computation.1 | async-start | bytes 1048576 | tf_op jit(solution)/shard_map/all_to_all | solution.py:514
  137.6 12.7 %collective-permute-start.18 = (bf16[8,1,8,128]{3,2,1,0:T(8,128)(2,1)S(1)}, bf16[8,1,8,128]{3,2,1,0:T(8,128)(2,1)S(1)}, u32[]{:S(2)}, u32[]{:S(2)}) collective-permute-start(bf16[8,1,8,128]{3,2,1,0:T(8,128)(2,1)S(1)} %get-tuple-element.102), channel_id=1, source_target_pairs={{0,1},{1,2},{2,3},{3,0},{4,5},{5,6},{6,7},{7,4},{8,9},{9,10},{10,1... | collective-permute-start | bytes 49160 | tf_op jit(solution)/shard_map/ppermute | solution.py:484
  139.1 11.3 %collective-permute-start.19 = (bf16[8,1,8,128]{3,2,1,0:T(8,128)(2,1)S(1)}, bf16[8,1,8,128]{3,2,1,0:T(8,128)(2,1)S(1)}, u32[]{:S(2)}, u32[]{:S(2)}) collective-permute-start(bf16[8,1,8,128]{3,2,1,0:T(8,128)(2,1)S(1)} %get-tuple-element.103), channel_id=1, source_target_pairs={{0,3},{1,0},{2,1},{3,2},{4,7},{5,4},{6,5},{7,6},{8,11},{9,8},{10,9... | collective-permute-start | bytes 49160 | tf_op jit(solution)/shard_map/ppermute | solution.py:484

commit v2 on v1

--- a/solution.py
+++ b/solution.py
@@ -44,19 +44,31 @@
     return sig + act * (1.0 - sig)
 
 
-def sort_kernel(latent_ref, bucket_ref, meta_ref, out_ref):
+def wrapped_step(target, mine, count):
+    step = target - mine.astype(F32) + 1.0
+    step = jnp.where(step < 0.0, step + count, step)
+    return jnp.where(step >= count, step - count, step)
+
+
+def sort_kernel(count_x, count_y, latent_ref, offset_ref, owner_ref, slot_ref, out_ref):
     rows = latent_ref.shape[0]
     send = rows // 9
-    bucket = bucket_ref[...]
-    hot = mask(iota((16, rows), 0) == bucket)
+    owner = owner_ref[...].astype(F32)
+    owner_x = jnp.floor((owner + 0.5) * (1.0 / count_y))
+    owner_y = owner - owner_x * count_y
+    bucket = 3.0 * wrapped_step(owner_x, lax.axis_index("gx"), count_x)
+    bucket = bucket + wrapped_step(owner_y, lax.axis_index("gy"), count_y)
+    hot = mask(iota((16, rows), 0).astype(F32) == bucket)
     upper = mask(iota((rows, rows), 0) <= iota((rows, rows), 1)).astype(BF)
     count = dot(hot.astype(BF), upper)
     rank = jnp.sum(hot * (count - 1.0), axis=0, keepdims=True)
-    target = bucket.astype(F32) * float(send) + rank
+    target = bucket * float(send) + rank
     perm = mask(iota((rows, rows), 0).astype(F32) == target).astype(BF)
     out_ref[:, :L] = dot(perm, latent_ref[...]).astype(BF)
-    meta = jnp.concatenate([meta_ref[...], jnp.zeros((L - 8, rows), F32)], axis=0).astype(BF)
-    out_ref[:, L:] = dot_nt(perm, meta).astype(BF)
+    mark = (slot_ref[...] + 1).astype(F32)
+    high = jnp.floor(mark * (1.0 / 16.0))
+    meta = [offset_ref[...].astype(F32), jnp.ones_like(mark), high, mark - 16.0 * high, jnp.zeros((L - 5, rows), F32)]
+    out_ref[:, L:] = dot_nt(perm, jnp.concatenate(meta, axis=0).astype(BF)).astype(BF)
 
 
 def place_kernel(rows_ref, pay_ref):
@@ -175,36 +187,57 @@
     return ref[pl.ds(first, 1), :], ref[pl.ds(first + 1, 1), :]
 
 
+def staggered(count, stages):
+    state = [{} for _ in range(count)]
+    for tick in range(count + len(stages) - 1):
+        for depth in range(len(stages)):
+            if 0 <= tick - depth < count:
+                stages[depth](tick - depth, state[tick - depth])
+
+
 def edges_forward(
     width, lhs_ref, weight_t_ref, far_ref, near_ref, shifts, g2, mid2_ref, bias2, sums_ref, wsum_ref, keep=None
 ):
     pairs = sums_ref.shape[0] // (2 * CAP)
+    group = 8
     col = iota((CAP, EDGES), 1)
     start = iota((CAP, EDGES), 0) * NEAR
     own = mask((col >= start) & (col < start + NEAR))
 
-    def body(pair, carry):
-        rhs = pair_rhs(pair, width, far_ref, near_ref, shifts, g2)
-        pre_one = dot(lhs_ref[...], rhs).astype(BF)
-        tanh_one = jnp.tanh(pre_one)
-        hidden = pre_one + pre_one * tanh_one
-        pre_two = (dot(hidden, mid2_ref[...]) + bias2).astype(BF)
-        tanh_two = jnp.tanh(pre_two)
-        act = pre_two + pre_two * tanh_two
-        if keep is not None:
-            at = pl.ds(pl.multiple_of(pair * EDGES, EDGES), EDGES)
-            keep[0][at, :] = hidden
-            keep[1][at, :] = slope_of(pre_one, tanh_one)
-            keep[2][at, :] = slope_of(pre_two, tanh_two)
-        row_a, row_b = pair_rows(pair, width, weight_t_ref)
-        spread = jnp.concatenate([own * row_a, own * row_b], axis=0)
-        sums = dot(spread.astype(BF), act)
-        at = pl.ds(pl.multiple_of(pair * 2 * CAP, 2 * CAP), 2 * CAP)
-        sums_ref[at, :] = jnp.concatenate([sums[:CAP, :L], sums[CAP:, L:]], axis=0)
-        wsum_ref[at, :] = jnp.broadcast_to(jnp.sum(spread, axis=1, keepdims=True), (2 * CAP, L))
+    def body(step, carry):
+        def first(k, s):
+            pair = step * group + k
+            rhs = pair_rhs(pair, width, far_ref, near_ref, shifts, g2)
+            pre_one = dot(lhs_ref[...], rhs).astype(BF)
+            tanh_one = jnp.tanh(pre_one)
+            s["hidden"] = pre_one + pre_one * tanh_one
+            if keep is not None:
+                at = pl.ds(pl.multiple_of(pair * EDGES, EDGES), EDGES)
+                keep[0][at, :] = s["hidden"]
+                keep[1][at, :] = slope_of(pre_one, tanh_one)
+
+        def second(k, s):
+            pair = step * group + k
+            pre_two = (dot(s["hidden"], mid2_ref[...]) + bias2).astype(BF)
+            tanh_two = jnp.tanh(pre_two)
+            s["act"] = pre_two + pre_two * tanh_two
+            if keep is not None:
+                at = pl.ds(pl.multiple_of(pair * EDGES, EDGES), EDGES)
+                keep[2][at, :] = slope_of(pre_two, tanh_two)
+
+        def third(k, s):
+            pair = step * group + k
+            row_a, row_b = pair_rows(pair, width, weight_t_ref)
+            spread = jnp.concatenate([own * row_a, own * row_b], axis=0)
+            sums = dot(spread.astype(BF), s["act"])
+            at = pl.ds(pl.multiple_of(pair * 2 * CAP, 2 * CAP), 2 * CAP)
+            sums_ref[at, :] = jnp.concatenate([sums[:CAP, :L], sums[CAP:, L:]], axis=0)
+            wsum_ref[at, :] = jnp.broadcast_to(jnp.sum(spread, axis=1, keepdims=True), (2 * CAP, L))
+
+        staggered(group, (first, second, third))
         return carry
 
-    lax.fori_loop(0, pairs, body, 0, unroll=4)
+    lax.fori_loop(0, pairs // group, body, 0)
 
 
 def edges_backward(
@@ -212,48 +245,61 @@
     d_sums_ref, d_own_ref, d_far_ref, mid_ref, rows_ref, bias_ref, keep=None,
 ):
     pairs = d_own_ref.shape[0] // (2 * CAP)
+    group = 8
     for ref in (d_far_ref, mid_ref, rows_ref, bias_ref):
         ref[...] = jnp.zeros_like(ref)
 
-    def body(pair, carry):
-        x, y = pair_place(pair, width - 2)
-        if keep is None:
+    def body(step, carry):
+        def first(k, s):
+            pair = step * group + k
             rhs = pair_rhs(pair, width, far_ref, near_ref, shifts, g2)
             pre_one = dot(lhs_ref[...], rhs).astype(BF)
             tanh_one = jnp.tanh(pre_one)
-            hidden = pre_one + pre_one * tanh_one
-            pre_two = (dot(hidden, mid2_ref[...]) + bias2).astype(BF)
-            slope_one = slope_of(pre_one, tanh_one)
-            slope_two = slope_of(pre_two, jnp.tanh(pre_two))
-        else:
-            at = pl.ds(pl.multiple_of(pair * EDGES, EDGES), EDGES)
-            hidden, slope_one, slope_two = (ref[at, :] for ref in keep)
-        pick = mask(pair_hot(pair, width)).astype(BF)
-        weight = dot(weight_ref[...], pick)
-        base = pl.multiple_of(pair * 2 * CAP, 2 * CAP)
-        d_sums = d_sums_ref[pl.ds(base, 2 * CAP), :]
-        d_sums = jnp.concatenate([d_sums[:CAP], d_sums[CAP:]], axis=1)
-        d_sums = jnp.broadcast_to(d_sums[:, None, :], (CAP, NEAR, 2 * L)).reshape(EDGES, 2 * L)
-        d_two = weight * d_sums * slope_two
-        bias_ref[...] += jnp.sum(d_two.reshape(EDGES // 8, 8, 2 * L), axis=0)
-        d_two = d_two.astype(BF)
-        mid_ref[...] += dot_tn(hidden, d_two)
-        d_one = (dot(d_two, mid2_t_ref[...]) * slope_one).astype(BF)
-        rad_a, rad_b = pair_rows(pair, width, radius_t_ref)
-        tail = jnp.concatenate([rad_a, rad_b, jnp.zeros((14, EDGES), F32)], axis=0).astype(BF)
-        back = dot(jnp.concatenate([hot_t_ref[...], tail], axis=0), d_one)
-        rows_ref[...] += back
-        own_rows = back[NEAR : NEAR + CAP]
-        d_own_ref[pl.ds(base, 2 * CAP), :] = jnp.concatenate([own_rows[:, :L], own_rows[:, L:]], axis=0)
-        for a in range(3):
-            piece = back[3 * CAP * a : 3 * CAP * (a + 1)]
-            zero = jnp.zeros((CAP, L), F32)
-            both = jnp.concatenate([piece[:, :L], zero], axis=0) + jnp.concatenate([zero, piece[:, L:]], axis=0)
-            at = pl.ds(pl.multiple_of(((x + a) * width + y) * CAP, CAP), 4 * CAP)
-            d_far_ref[at, :] += both
+            s["hidden"] = pre_one + pre_one * tanh_one
+            s["slope"] = slope_of(pre_one, tanh_one)
+
+        def second(k, s):
+            pair = step * group + k
+            if keep is None:
+                pre_two = (dot(s["hidden"], mid2_ref[...]) + bias2).astype(BF)
+                slope_two = slope_of(pre_two, jnp.tanh(pre_two))
+            else:
+                at = pl.ds(pl.multiple_of(pair * EDGES, EDGES), EDGES)
+                s["hidden"], s["slope"], slope_two = (ref[at, :] for ref in keep)
+            pick = mask(pair_hot(pair, width)).astype(BF)
+            weight = dot(weight_ref[...], pick)
+            d_sums = d_sums_ref[pl.ds(pl.multiple_of(pair * 2 * CAP, 2 * CAP), 2 * CAP), :]
+            d_sums = jnp.concatenate([d_sums[:CAP], d_sums[CAP:]], axis=1)
+            d_sums = jnp.broadcast_to(d_sums[:, None, :], (CAP, NEAR, 2 * L)).reshape(EDGES, 2 * L)
+            d_two = weight * d_sums * slope_two
+            bias_ref[...] += jnp.sum(d_two.reshape(EDGES // 8, 8, 2 * L), axis=0)
+            s["two"] = d_two.astype(BF)
+
+        def third(k, s):
+            mid_ref[...] += dot_tn(s["hidden"], s["two"])
+            s["one"] = (dot(s["two"], mid2_t_ref[...]) * s["slope"]).astype(BF)
+
+        def fourth(k, s):
+            pair = step * group + k
+            x, y = pair_place(pair, width - 2)
+            rad_a, rad_b = pair_rows(pair, width, radius_t_ref)
+            tail = jnp.concatenate([rad_a, rad_b, jnp.zeros((14, EDGES), F32)], axis=0).astype(BF)
+            back = dot(jnp.concatenate([hot_t_ref[...], tail], axis=0), s["one"])
+            rows_ref[...] += back
+            own_rows = back[NEAR : NEAR + CAP]
+            at = pl.ds(pl.multiple_of(pair * 2 * CAP, 2 * CAP), 2 * CAP)
+            d_own_ref[at, :] = jnp.concatenate([own_rows[:, :L], own_rows[:, L:]], axis=0)
+            for a in range(3):
+                piece = back[3 * CAP * a : 3 * CAP * (a + 1)]
+                zero = jnp.zeros((CAP, L), F32)
+                both = jnp.concatenate([piece[:, :L], zero], axis=0) + jnp.concatenate([zero, piece[:, L:]], axis=0)
+                at = pl.ds(pl.multiple_of(((x + a) * width + y) * CAP, CAP), 4 * CAP)
+                d_far_ref[at, :] += both
+
+        staggered(group, (second, third, fourth) if keep is not None else (first, second, third, fourth))
         return carry
 
-    lax.fori_loop(0, pairs, body, 0, unroll=4)
+    lax.fori_loop(0, pairs // group, body, 0)
 
 
 def geo_grads(rows, d_far, geo_halo, d_own, geo_own):
@@ -523,23 +569,12 @@
     halo_rows = (cells_x + 2) * width * cap_size
     count_x = lax.axis_size("gx")
     count_y = lax.axis_size("gy")
-    my_x = lax.axis_index("gx")
-    my_y = lax.axis_index("gy")
     rows = latent.shape[0]
     send = rows // 9
-    step_x = (owner // count_y - my_x + 1) % count_x
-    step_y = (owner % count_y - my_y + 1) % count_y
-    bucket = (step_x * 3 + step_y)[None, :]
-    mark = slot + 1
-    ones = jnp.ones((rows,), F32)
-    zeros = jnp.zeros((rows,), F32)
-    meta = jnp.stack(
-        [
-            offset[0].astype(F32), offset[1].astype(F32), ones, (mark // 16).astype(F32), (mark % 16).astype(F32),
-            zeros, zeros, zeros,
-        ]
-    )
-    (sent,) = call(sort_kernel, [((rows, 2 * L), BF)], [], latent, bucket, meta)
+    (sent,) = call(
+        functools.partial(sort_kernel, count_x, count_y), [((rows, 2 * L), BF)], [],
+        latent, offset, owner[None, :], slot[None, :],
+    )
     sent = sent.reshape(3, 3, send, 2 * L)
     sections = [sent[:, 1], from_behind(sent[:, 2], "gy", 1), from_behind(sent[:, 0], "gy", -1)]
     section = jnp.stack(sections)

time: 156 us -> 146 us (0.936)
  Pallas kernels: 64.8 us -> 55.3 us
    pallas_call x7, Pallas kernels: 64.8 us -> 55.3 us  [call(): pl.pallas_call(kernel, out_shape=[jax.ShapeDtypeStruct(shape, dtype) for...]
where the time goes in v2:
time: 146 us
  Pallas kernels  55.3 us (38%)
  starting transfers between devices  43 us (29%)
  waiting for transfers between devices  39.5 us (27%)
  local copies, waits for them, and re-layouts  5.81 us (4%)
    pallas_call x7, Pallas kernels, call(): pl.pallas_call(kernel, out_shape=[jax.ShapeDtypeStruct(shape, dtype) for...  55.3 us
    ppermute x20, starting transfers between devices, from_behind(): lax.ppermute(value, axis, [(source, (source + steps) % count) for source...  31.5 us
    ppermute x20, waiting for transfers between devices, from_behind(): lax.ppermute(value, axis, [(source, (source + steps) % count) for source...  23.9 us
    all_to_all x1, waiting for transfers between devices, total_over_devices(): parts = lax.all_to_all(rows.reshape(count, -1, L), axes, 0, 0)  13.5 us
    all_to_all x1, starting transfers between devices, total_over_devices(): parts = lax.all_to_all(rows.reshape(count, -1, L), axes, 0, 0)  8.31 us
    unnamed x30, local copies, waits for them, and re-layouts  4.77 us
    all_to_all x1, starting transfers between devices, total_over_devices(): return lax.all_to_all(spread, axes, 0, 0).reshape(-1, L)  3.15 us
  transfers between devices with their start and end apart: 22, of which 15 were waited for; matrix products, arithmetic and copies ran while one was open for 1% of the time, Pallas kernels for 1%

profile of v2, /device:TPU:1, one launch (start us, length us, event | category | flops | bytes accessed | tf_op | source)
XLA Modules:
  0.0 145.9 jit_solution(8655953364441649411)
XLA Ops:
  0.7 0.7 copy-done.8
  1.3 0.9 copy-done.6
  2.2 0.7 copy-done.9
  2.9 0.7 copy-done.10
  3.6 0.6 shard_map.204
  4.2 2.2 %collective-permute-start = (bf16[3,48,256]{2,1,0:T(8,128)(2,1)S(1)}, bf16[3,48,256]{2,1,0:T(8,128)(2,1)S(1)}, u32[]{:S(2)}, u32[]{:S(2)}) collective-permute-start(bf16[3,48,256]{2,1,0:T(8,128)(2,1)S(1)} %get-tuple-element.96), channel_id=1, source_target_pairs={{0,1},{1,2},{2,3},{3,0},{4,5},{5,6},{6,7},{7,4},{8,9},{9,10},{10,1... | collective-permute-start | bytes 221192 | tf_op jit(solution)/shard_map/ppermute | solution.py:530
  6.4 2.1 %collective-permute-start.1 = (bf16[3,48,256]{2,1,0:T(8,128)(2,1)S(1)}, bf16[3,48,256]{2,1,0:T(8,128)(2,1)S(1)}, u32[]{:S(2)}, u32[]{:S(2)}) collective-permute-start(bf16[3,48,256]{2,1,0:T(8,128)(2,1)S(1)} %get-tuple-element.97), channel_id=1, source_target_pairs={{0,3},{1,0},{2,1},{3,2},{4,7},{5,4},{6,5},{7,6},{8,11},{9,8},{10,9... | collective-permute-start | bytes 221192 | tf_op jit(solution)/shard_map/ppermute | solution.py:530
  8.5 1.8 %collective-permute-done = bf16[3,48,256]{2,1,0:T(8,128)(2,1)S(1)} collective-permute-done((bf16[3,48,256]{2,1,0:T(8,128)(2,1)S(1)}, bf16[3,48,256]{2,1,0:T(8,128)(2,1)S(1)}, u32[]{:S(2)}, u32[]{:S(2)}) %collective-permute-start) | collective-permute-done | bytes 73760 | tf_op jit(solution)/shard_map/ppermute | solution.py:530
  10.2 1.3 collective-permute-done.1
  11.6 1.1 collective-permute-start.3
  12.7 1.2 collective-permute-start.2
  13.9 2.0 %collective-permute-done.3 = bf16[3,48,256]{2,1,0:T(8,128)(2,1)S(1)} collective-permute-done((bf16[3,48,256]{2,1,0:T(8,128)(2,1)S(1)}, bf16[3,48,256]{2,1,0:T(8,128)(2,1)S(1)}, u32[]{:S(2)}, u32[]{:S(2)}) %collective-permute-start.3) | collective-permute-done | bytes 73760 | tf_op jit(solution)/shard_map/ppermute | solution.py:530
  16.3 2.4 %collective-permute-start.4 = (bf16[1,8,8,256]{3,2,1,0:T(8,128)(2,1)S(1)}, bf16[1,8,8,256]{3,2,1,0:T(8,128)(2,1)S(1)}, u32[]{:S(2)}, u32[]{:S(2)}) collective-permute-start(bf16[1,8,8,256]{3,2,1,0:T(8,128)(2,1)S(1)} %get-tuple-element.90), channel_id=1, source_target_pairs={{0,4},{4,8},{8,12},{12,16},{16,20},{20,24},{24,28},{28,0},{1,5},{5... | collective-permute-start | bytes 98312 | tf_op jit(solution)/shard_map/ppermute | solution.py:530
  19.2 0.6 collective-permute-done.4
  19.8 2.3 %collective-permute-done.5 = bf16[1,8,8,256]{3,2,1,0:T(8,128)(2,1)S(1)} collective-permute-done((bf16[1,8,8,256]{3,2,1,0:T(8,128)(2,1)S(1)}, bf16[1,8,8,256]{3,2,1,0:T(8,128)(2,1)S(1)}, u32[]{:S(2)}, u32[]{:S(2)}) %collective-permute-start.5) | collective-permute-done | bytes 32800 | tf_op jit(solution)/shard_map/ppermute | solution.py:530
  22.6 2.9 %collective-permute-start.7 = (bf16[10,1,8,256]{3,2,1,0:T(8,128)(2,1)S(1)}, bf16[10,1,8,256]{3,2,1,0:T(8,128)(2,1)S(1)}, u32[]{:S(2)}, u32[]{:S(2)}) collective-permute-start(bf16[10,1,8,256]{3,2,1,0:T(8,128)(2,1)S(1)} %get-tuple-element.89), channel_id=1, source_target_pairs={{0,3},{1,0},{2,1},{3,2},{4,7},{5,4},{6,5},{7,6},{8,11},{9,8},{10,9... | collective-permute-start | bytes 122888 | tf_op jit(solution)/shard_map/ppermute | solution.py:530
  25.6 1.4 collective-permute-done.6
  27.1 0.6 copy-done.7
  27.7 9.4 %shard_map.206 = (bf16[576,256]{1,0:T(8,128)(2,1)S(1)}, bf16[576,128]{1,0:T(8,128)(2,1)S(1)}, f32[128,576]{1,0:T(8,128)S(1)}, f32[128,576]{1,0:T(8,128)S(1)}, bf...) custom-call(bf16[800,256]{1,0:T(8,128)(2,1)S(1)} %bitcast.63, ...), custom_call_target="tpu_custom_call" | custom-call | tf_op jit(solution)/shard_map/pallas_call | solution.py:518
  37.2 1.2 collective-permute-start.8
  38.4 1.6 %collective-permute-start.9 = (bf16[1,8,8,128]{3,2,1,0:T(8,128)(2,1)S(1)}, bf16[1,8,8,128]{3,2,1,0:T(8,128)(2,1)S(1)}, u32[]{:S(2)}, u32[]{:S(2)}) collective-permute-start(bf16[1,8,8,128]{3,2,1,0:T(8,128)(2,1)S(1)} %get-tuple-element.109), channel_id=1, source_target_pairs={{0,28},{4,0},{8,4},{12,8},{16,12},{20,16},{24,20},{28,24},{1,29},{... | collective-permute-start | bytes 49160 | tf_op jit(solution)/shard_map/ppermute | solution.py:530
  40.0 0.6 collective-permute-done.8
  40.6 1.0 collective-permute-done.9
  41.6 0.6 collective-permute-start.10
  42.2 3.3 %collective-permute-start.11 = (bf16[10,1,8,128]{3,2,1,0:T(8,128)(2,1)S(1)}, bf16[10,1,8,128]{3,2,1,0:T(8,128)(2,1)S(1)}, u32[]{:S(2)}, u32[]{:S(2)}) collective-permute-start(bf16[10,1,8,128]{3,2,1,0:T(8,128)(2,1)S(1)} %get-tuple-element.107), channel_id=1, source_target_pairs={{0,3},{1,0},{2,1},{3,2},{4,7},{5,4},{6,5},{7,6},{8,11},{9,8},{10,9... | collective-permute-start | bytes 61448 | tf_op jit(solution)/shard_map/ppermute | solution.py:530
  45.5 0.9 collective-permute-done.10
  46.4 23.9 %shard_map.207 = (bf16[512,128]{1,0:T(8,128)(2,1)}, f32[512,128]{1,0:T(8,128)S(1)}, f32[800,128]{1,0:T(8,128)S(1)}, f32[512,128]{1,0:T(8,128)S(1)}, bf16[1024,128]{1,0:T(8,128)(2,1)S(1)}) custom-call(bf16[800,128]{1,0:T(8,128)(2,1)S(1)} %bitcast.72, bf16[800,256]{1,0:T(8,128)(2,1)S(1)} %bitcast.64, bf16[512,256]{1,0:T(8,128)(2,1)S(1)} %shard_map.205.pay_ref, ...), custom_call_target="tpu_custom_call" | custom-call | tf_op jit(solution)/shard_map/pallas_call | solution.py:518
  70.4 1.6 %collective-permute-start.12 = (bf16[1,10,8,128]{3,2,1,0:T(8,128)(2,1)S(1)}, bf16[1,10,8,128]{3,2,1,0:T(8,128)(2,1)S(1)}, u32[]{:S(2)}, u32[]{:S(2)}) collective-permute-start(bf16[1,10,8,128]{3,2,1,0:T(8,128)(2,1)S(1)} %get-tuple-element.100), channel_id=1, source_target_pairs={{0,4},{4,8},{8,12},{12,16},{16,20},{20,24},{24,28},{28,0},{1,5},{5... | collective-permute-start | bytes 61448 | tf_op jit(solution)/shard_map/ppermute | solution.py:530
  72.0 1.8 %collective-permute-start.13 = (bf16[1,10,8,128]{3,2,1,0:T(8,128)(2,1)S(1)}, bf16[1,10,8,128]{3,2,1,0:T(8,128)(2,1)S(1)}, u32[]{:S(2)}, u32[]{:S(2)}) collective-permute-start(bf16[1,10,8,128]{3,2,1,0:T(8,128)(2,1)S(1)} %get-tuple-element.101), channel_id=1, source_target_pairs={{0,28},{4,0},{8,4},{12,8},{16,12},{20,16},{24,20},{28,24},{1,29},{... | collective-permute-start | bytes 61448 | tf_op jit(solution)/shard_map/ppermute | solution.py:530
  73.8 0.6 collective-permute-done.12
  74.4 1.3 collective-permute-done.13
  76.3 3.2 %collective-permute-start.15 = (bf16[8,1,8,128]{3,2,1,0:T(8,128)(2,1)S(1)}, bf16[8,1,8,128]{3,2,1,0:T(8,128)(2,1)S(1)}, u32[]{:S(2)}, u32[]{:S(2)}) collective-permute-start(bf16[8,1,8,128]{3,2,1,0:T(8,128)(2,1)S(1)} %get-tuple-element.105), channel_id=1, source_target_pairs={{0,3},{1,0},{2,1},{3,2},{4,7},{5,4},{6,5},{7,6},{8,11},{9,8},{10,9... | collective-permute-start | bytes 49160 | tf_op jit(solution)/shard_map/ppermute | solution.py:530
  79.5 0.8 collective-permute-done.14
  80.4 19.0 %shard_map.208 = (f32[512,128]{1,0:T(8,128)S(1)}, f32[800,128]{1,0:T(8,128)S(1)}, f32[512,128]{1,0:T(8,128)S(1)}, bf16[1024,128]{1,0:T(8,128)(2,1)S(1)}) custom-call(f32[512,128]{1,0:T(8,128)S(1)} %get-tuple-element.47.next_d_own_ref, f32[512,128]{1,0:T(8,128)S(1)} %bitcast.69, f32[512,128]{1,0:T(8,128)S(1)} %get-tuple-element.49.next_grad_ref, ...), custom_call_target="tpu_custom_call" | custom-call | tf_op jit(solution)/shard_map/pallas_call | solution.py:518
  99.4 0.8 pad_maximum_fusion
  100.3 8.3 %all-to-all-start = ((bf16[32,64,128]{2,1,0:T(8,128)(2,1)}), bf16[32,64,128]{2,1,0:T(8,128)(2,1)S(1)}, u32[]{:S(2)}, u32[]{:S(2)}) async-start(bf16[32,64,128]{2,1,0:T(8,128)(2,1)} %bitcast.36), calls=%async_computation | async-start | bytes 1048576 | tf_op jit(solution)/shard_map/all_to_all | solution.py:557
  108.6 1.7 %collective-permute-start.16 = (bf16[1,10,8,128]{3,2,1,0:T(8,128)(2,1)S(1)}, bf16[1,10,8,128]{3,2,1,0:T(8,128)(2,1)S(1)}, u32[]{:S(2)}, u32[]{:S(2)}) collective-permute-start(bf16[1,10,8,128]{3,2,1,0:T(8,128)(2,1)S(1)} %get-tuple-element.98), channel_id=1, source_target_pairs={{0,4},{4,8},{8,12},{12,16},{16,20},{20,24},{24,28},{28,0},{1,5},{5... | collective-permute-start | bytes 61448 | tf_op jit(solution)/shard_map/ppermute | solution.py:530
  110.3 13.5 %all-to-all-done = bf16[32,64,128]{2,1,0:T(8,128)(2,1)S(1)} async-done(((bf16[32,64,128]{2,1,0:T(8,128)(2,1)}), bf16[32,64,128]{2,1,0:T(8,128)(2,1)S(1)}, u32[]{:S(2)}, u32[]{:S(2)}) %all-to-all-start) | async-done | bytes 524320 | tf_op jit(solution)/shard_map/all_to_all | solution.py:557
  123.9 0.9 broadcast_in_dim.14
  124.8 3.2 %all-to-all-start.1 = ((bf16[32,64,128]{2,1,0:T(8,128)(2,1)}), bf16[32,64,128]{2,1,0:T(8,128)(2,1)S(1)}, u32[]{:S(2)}, u32[]{:S(2)}) async-start(bf16[32,64,128]{2,1,0:T(8,128)(2,1)} %broadcast_in_dim.14), calls=%async_computation.1 | async-start | bytes 1048576 | tf_op jit(solution)/shard_map/all_to_all | solution.py:560
  128.1 1.4 collective-permute-start.18
  129.5 1.9 %collective-permute-start.19 = (bf16[8,1,8,128]{3,2,1,0:T(8,128)(2,1)S(1)}, bf16[8,1,8,128]{3,2,1,0:T(8,128)(2,1)S(1)}, u32[]{:S(2)}, u32[]{:S(2)}) collective-permute-start(bf16[8,1,8,128]{3,2,1,0:T(8,128)(2,1)S(1)} %get-tuple-element.103), channel_id=1, source_target_pairs={{0,3},{1,0},{2,1},{3,2},{4,7},{5,4},{6,5},{7,6},{8,11},{9,8},{10,9... | collective-permute-start | bytes 49160 | tf_op jit(solution)/shard_map/ppermute | solution.py:530
  131.5 9.3 %collective-permute-done.18 = bf16[8,1,8,128]{3,2,1,0:T(8,128)(2,1)S(1)} collective-permute-done((bf16[8,1,8,128]{3,2,1,0:T(8,128)(2,1)S(1)}, bf16[8,1,8,128]{3,2,1,0:T(8,128)(2,1)S(1)}, u32[]{:S(2)}, u32[]{:S(2)}) %collective-permute-start.18) | collective-permute-done | bytes 16416 | tf_op jit(solution)/shard_map/ppermute | solution.py:530
  140.8 0.9 shard_map.209
  141.8 2.0 %all-to-all-done.1 = bf16[32,64,128]{2,1,0:T(8,128)(2,1)S(1)} async-done(((bf16[32,64,128]{2,1,0:T(8,128)(2,1)}), bf16[32,64,128]{2,1,0:T(8,128)(2,1)S(1)}, u32[]{:S(2)}, u32[]{:S(2)}) %all-to-all-start.1) | async-done | bytes 524320 | tf_op jit(solution)/shard_map/all_to_all | solution.py:560
  143.8 0.9 shard_map.210
  144.7 0.6 copy.32
  145.3 0.6 copy.33
  (66 shorter events, 2.6 us)
Async XLA Ops:
  0.6 0.7 copy-start.8
  1.3 0.9 copy-start.6
  2.2 0.7 copy-start.9
  2.9 0.7 copy-start.10
  4.2 6.0 %collective-permute-start = (bf16[3,48,256]{2,1,0:T(8,128)(2,1)S(1)}, bf16[3,48,256]{2,1,0:T(8,128)(2,1)S(1)}, u32[]{:S(2)}, u32[]{:S(2)}) collective-permute-start(bf16[3,48,256]{2,1,0:T(8,128)(2,1)S(1)} %get-tuple-element.96), channel_id=1, source_target_pairs={{0,1},{1,2},{2,3},{3,0},{4,5},{5,6},{6,7},{7,4},{8,9},{9,10},{10,1... | collective-permute-start | bytes 221192 | tf_op jit(solution)/shard_map/ppermute | solution.py:530
  6.4 5.2 %collective-permute-start.1 = (bf16[3,48,256]{2,1,0:T(8,128)(2,1)S(1)}, bf16[3,48,256]{2,1,0:T(8,128)(2,1)S(1)}, u32[]{:S(2)}, u32[]{:S(2)}) collective-permute-start(bf16[3,48,256]{2,1,0:T(8,128)(2,1)S(1)} %get-tuple-element.97), channel_id=1, source_target_pairs={{0,3},{1,0},{2,1},{3,2},{4,7},{5,4},{6,5},{7,6},{8,11},{9,8},{10,9... | collective-permute-start | bytes 221192 | tf_op jit(solution)/shard_map/ppermute | solution.py:530
  11.6 4.3 %collective-permute-start.3 = (bf16[3,48,256]{2,1,0:T(8,128)(2,1)S(1)}, bf16[3,48,256]{2,1,0:T(8,128)(2,1)S(1)}, u32[]{:S(2)}, u32[]{:S(2)}) collective-permute-start(bf16[3,48,256]{2,1,0:T(8,128)(2,1)S(1)} %get-tuple-element.93), channel_id=1, source_target_pairs={{0,28},{4,0},{8,4},{12,8},{16,12},{20,16},{24,20},{28,24},{1,29},{... | collective-permute-start | bytes 221192 | tf_op jit(solution)/shard_map/ppermute | solution.py:530
  12.7 3.1 %collective-permute-start.2 = (bf16[3,48,256]{2,1,0:T(8,128)(2,1)S(1)}, bf16[3,48,256]{2,1,0:T(8,128)(2,1)S(1)}, u32[]{:S(2)}, u32[]{:S(2)}) collective-permute-start(bf16[3,48,256]{2,1,0:T(8,128)(2,1)S(1)} %get-tuple-element.94), channel_id=1, source_target_pairs={{0,4},{4,8},{8,12},{12,16},{16,20},{20,24},{24,28},{28,0},{1,5},{5... | collective-permute-start | bytes 221192 | tf_op jit(solution)/shard_map/ppermute | solution.py:530
  16.3 3.5 %collective-permute-start.4 = (bf16[1,8,8,256]{3,2,1,0:T(8,128)(2,1)S(1)}, bf16[1,8,8,256]{3,2,1,0:T(8,128)(2,1)S(1)}, u32[]{:S(2)}, u32[]{:S(2)}) collective-permute-start(bf16[1,8,8,256]{3,2,1,0:T(8,128)(2,1)S(1)} %get-tuple-element.90), channel_id=1, source_target_pairs={{0,4},{4,8},{8,12},{12,16},{16,20},{20,24},{24,28},{28,0},{1,5},{5... | collective-permute-start | bytes 98312 | tf_op jit(solution)/shard_map/ppermute | solution.py:530
  18.8 3.3 %collective-permute-start.5 = (bf16[1,8,8,256]{3,2,1,0:T(8,128)(2,1)S(1)}, bf16[1,8,8,256]{3,2,1,0:T(8,128)(2,1)S(1)}, u32[]{:S(2)}, u32[]{:S(2)}) collective-permute-start(bf16[1,8,8,256]{3,2,1,0:T(8,128)(2,1)S(1)} %get-tuple-element.91), channel_id=1, source_target_pairs={{0,28},{4,0},{8,4},{12,8},{16,12},{20,16},{24,20},{28,24},{1,29},{... | collective-permute-start | bytes 98312 | tf_op jit(solution)/shard_map/ppermute | solution.py:530
  22.1 3.3 %copy-start.12 = (bf16[2,3,128]{2,0,1:T(2,128)(2,1)S(1)}, bf16[2,3,128]{2,0,1:T(2,128)(2,1)}, u32[]{:S(2)}) copy-start(bf16[2,3,128]{2,0,1:T(2,128)(2,1)} %param.19) | copy-start | bytes 4612
  22.2 3.3 %copy-start.11 = (bf16[2,5,128]{2,0,1:T(2,128)(2,1)S(1)}, bf16[2,5,128]{2,0,1:T(2,128)(2,1)}, u32[]{:S(2)}) copy-start(bf16[2,5,128]{2,0,1:T(2,128)(2,1)} %param.24) | copy-start | bytes 7684
  22.2 4.8 %collective-permute-start.6 = (bf16[10,1,8,256]{3,2,1,0:T(8,128)(2,1)S(1)}, bf16[10,1,8,256]{3,2,1,0:T(8,128)(2,1)S(1)}, u32[]{:S(2)}, u32[]{:S(2)}) collective-permute-start(bf16[10,1,8,256]{3,2,1,0:T(8,128)(2,1)S(1)} %get-tuple-element.88), channel_id=1, source_target_pairs={{0,1},{1,2},{2,3},{3,0},{4,5},{5,6},{6,7},{7,4},{8,9},{9,10},{10,1... | collective-permute-start | bytes 122888 | tf_op jit(solution)/shard_map/ppermute | solution.py:530
  22.6 4.4 %collective-permute-start.7 = (bf16[10,1,8,256]{3,2,1,0:T(8,128)(2,1)S(1)}, bf16[10,1,8,256]{3,2,1,0:T(8,128)(2,1)S(1)}, u32[]{:S(2)}, u32[]{:S(2)}) collective-permute-start(bf16[10,1,8,256]{3,2,1,0:T(8,128)(2,1)S(1)} %get-tuple-element.89), channel_id=1, source_target_pairs={{0,3},{1,0},{2,1},{3,2},{4,7},{5,4},{6,5},{7,6},{8,11},{9,8},{10,9... | collective-permute-start | bytes 122888 | tf_op jit(solution)/shard_map/ppermute | solution.py:530
  25.5 1.6 %copy-start = (bf16[2,128,256]{2,1,0:T(8,128)(2,1)S(1)}, bf16[2,128,256]{2,1,0:T(8,128)(2,1)}, u32[]{:S(2)}) copy-start(bf16[2,128,256]{2,1,0:T(8,128)(2,1)} %edge_in_ref.1) | copy-start | bytes 393220
  25.5 1.6 %copy-start.1 = (bf16[2,256,128]{2,1,0:T(8,128)(2,1)S(1)}, bf16[2,256,128]{2,1,0:T(8,128)(2,1)}, u32[]{:S(2)}) copy-start(bf16[2,256,128]{2,1,0:T(8,128)(2,1)} %refs_15_.1) | copy-start | bytes 393220
  25.5 1.6 %copy-start.2 = (bf16[2,128,128]{2,1,0:T(8,128)(2,1)S(1)}, bf16[2,128,128]{2,1,0:T(8,128)(2,1)}, u32[]{:S(2)}) copy-start(bf16[2,128,128]{2,1,0:T(8,128)(2,1)} %refs_13_.1) | copy-start | bytes 196612
  25.5 1.6 %copy-start.3 = (bf16[2,128,128]{2,1,0:T(8,128)(2,1)S(1)}, bf16[2,128,128]{2,1,0:T(8,128)(2,1)}, u32[]{:S(2)}) copy-start(bf16[2,128,128]{2,1,0:T(8,128)(2,1)} %refs_14_.1) | copy-start | bytes 196612
  25.6 1.6 %copy-start.4 = (bf16[2,128,128]{2,1,0:T(8,128)(2,1)S(1)}, bf16[2,128,128]{2,1,0:T(8,128)(2,1)}, u32[]{:S(2)}) copy-start(bf16[2,128,128]{2,1,0:T(8,128)(2,1)} %refs_16_.1) | copy-start | bytes 196612
  27.1 0.7 copy-start.7
  37.2 3.4 %collective-permute-start.8 = (bf16[1,8,8,128]{3,2,1,0:T(8,128)(2,1)S(1)}, bf16[1,8,8,128]{3,2,1,0:T(8,128)(2,1)S(1)}, u32[]{:S(2)}, u32[]{:S(2)}) collective-permute-start(bf16[1,8,8,128]{3,2,1,0:T(8,128)(2,1)S(1)} %get-tuple-element.108), channel_id=1, source_target_pairs={{0,4},{4,8},{8,12},{12,16},{16,20},{20,24},{24,28},{28,0},{1,5},{5... | collective-permute-start | bytes 49160 | tf_op jit(solution)/shard_map/ppermute | solution.py:530
  38.4 3.2 %collective-permute-start.9 = (bf16[1,8,8,128]{3,2,1,0:T(8,128)(2,1)S(1)}, bf16[1,8,8,128]{3,2,1,0:T(8,128)(2,1)S(1)}, u32[]{:S(2)}, u32[]{:S(2)}) collective-permute-start(bf16[1,8,8,128]{3,2,1,0:T(8,128)(2,1)S(1)} %get-tuple-element.109), channel_id=1, source_target_pairs={{0,28},{4,0},{8,4},{12,8},{16,12},{20,16},{24,20},{28,24},{1,29},{... | collective-permute-start | bytes 49160 | tf_op jit(solution)/shard_map/ppermute | solution.py:530
  41.6 4.8 %collective-permute-start.10 = (bf16[10,1,8,128]{3,2,1,0:T(8,128)(2,1)S(1)}, bf16[10,1,8,128]{3,2,1,0:T(8,128)(2,1)S(1)}, u32[]{:S(2)}, u32[]{:S(2)}) collective-permute-start(bf16[10,1,8,128]{3,2,1,0:T(8,128)(2,1)S(1)} %get-tuple-element.106), channel_id=1, source_target_pairs={{0,1},{1,2},{2,3},{3,0},{4,5},{5,6},{6,7},{7,4},{8,9},{9,10},{10,1... | collective-permute-start | bytes 61448 | tf_op jit(solution)/shard_map/ppermute | solution.py:530
  42.2 4.2 %copy-start.5 = (bf16[8,8,8,128]{3,2,1,0:T(8,128)(2,1)S(1)}, bf16[8,8,8,128]{3,2,1,0:T(8,128)(2,1)}, u32[]{:S(2)}) copy-start(bf16[8,8,8,128]{3,2,1,0:T(8,128)(2,1)} %param.17) | copy-start | bytes 393220
  42.2 4.2 %collective-permute-start.11 = (bf16[10,1,8,128]{3,2,1,0:T(8,128)(2,1)S(1)}, bf16[10,1,8,128]{3,2,1,0:T(8,128)(2,1)S(1)}, u32[]{:S(2)}, u32[]{:S(2)}) collective-permute-start(bf16[10,1,8,128]{3,2,1,0:T(8,128)(2,1)S(1)} %get-tuple-element.107), channel_id=1, source_target_pairs={{0,3},{1,0},{2,1},{3,2},{4,7},{5,4},{6,5},{7,6},{8,11},{9,8},{10,9... | collective-permute-start | bytes 61448 | tf_op jit(solution)/shard_map/ppermute | solution.py:530
  70.4 4.0 %collective-permute-start.12 = (bf16[1,10,8,128]{3,2,1,0:T(8,128)(2,1)S(1)}, bf16[1,10,8,128]{3,2,1,0:T(8,128)(2,1)S(1)}, u32[]{:S(2)}, u32[]{:S(2)}) collective-permute-start(bf16[1,10,8,128]{3,2,1,0:T(8,128)(2,1)S(1)} %get-tuple-element.100), channel_id=1, source_target_pairs={{0,4},{4,8},{8,12},{12,16},{16,20},{20,24},{24,28},{28,0},{1,5},{5... | collective-permute-start | bytes 61448 | tf_op jit(solution)/shard_map/ppermute | solution.py:530
  72.0 3.7 %collective-permute-start.13 = (bf16[1,10,8,128]{3,2,1,0:T(8,128)(2,1)S(1)}, bf16[1,10,8,128]{3,2,1,0:T(8,128)(2,1)S(1)}, u32[]{:S(2)}, u32[]{:S(2)}) collective-permute-start(bf16[1,10,8,128]{3,2,1,0:T(8,128)(2,1)S(1)} %get-tuple-element.101), channel_id=1, source_target_pairs={{0,28},{4,0},{8,4},{12,8},{16,12},{20,16},{24,20},{28,24},{1,29},{... | collective-permute-start | bytes 61448 | tf_op jit(solution)/shard_map/ppermute | solution.py:530
  75.7 4.6 %collective-permute-start.14 = (bf16[8,1,8,128]{3,2,1,0:T(8,128)(2,1)S(1)}, bf16[8,1,8,128]{3,2,1,0:T(8,128)(2,1)S(1)}, u32[]{:S(2)}, u32[]{:S(2)}) collective-permute-start(bf16[8,1,8,128]{3,2,1,0:T(8,128)(2,1)S(1)} %get-tuple-element.104), channel_id=1, source_target_pairs={{0,1},{1,2},{2,3},{3,0},{4,5},{5,6},{6,7},{7,4},{8,9},{9,10},{10,1... | collective-permute-start | bytes 49160 | tf_op jit(solution)/shard_map/ppermute | solution.py:530
  76.3 4.1 %collective-permute-start.15 = (bf16[8,1,8,128]{3,2,1,0:T(8,128)(2,1)S(1)}, bf16[8,1,8,128]{3,2,1,0:T(8,128)(2,1)S(1)}, u32[]{:S(2)}, u32[]{:S(2)}) collective-permute-start(bf16[8,1,8,128]{3,2,1,0:T(8,128)(2,1)S(1)} %get-tuple-element.105), channel_id=1, source_target_pairs={{0,3},{1,0},{2,1},{3,2},{4,7},{5,4},{6,5},{7,6},{8,11},{9,8},{10,9... | collective-permute-start | bytes 49160 | tf_op jit(solution)/shard_map/ppermute | solution.py:530
  100.3 23.6 %all-to-all-start = ((bf16[32,64,128]{2,1,0:T(8,128)(2,1)}), bf16[32,64,128]{2,1,0:T(8,128)(2,1)S(1)}, u32[]{:S(2)}, u32[]{:S(2)}) async-start(bf16[32,64,128]{2,1,0:T(8,128)(2,1)} %bitcast.36), calls=%async_computation | async-start | bytes 1048576 | tf_op jit(solution)/shard_map/all_to_all | solution.py:557
  108.6 19.4 %collective-permute-start.16 = (bf16[1,10,8,128]{3,2,1,0:T(8,128)(2,1)S(1)}, bf16[1,10,8,128]{3,2,1,0:T(8,128)(2,1)S(1)}, u32[]{:S(2)}, u32[]{:S(2)}) collective-permute-start(bf16[1,10,8,128]{3,2,1,0:T(8,128)(2,1)S(1)} %get-tuple-element.98), channel_id=1, source_target_pairs={{0,4},{4,8},{8,12},{12,16},{16,20},{20,24},{24,28},{28,0},{1,5},{5... | collective-permute-start | bytes 61448 | tf_op jit(solution)/shard_map/ppermute | solution.py:530
  110.3 17.7 %collective-permute-start.17 = (bf16[1,10,8,128]{3,2,1,0:T(8,128)(2,1)S(1)}, bf16[1,10,8,128]{3,2,1,0:T(8,128)(2,1)S(1)}, u32[]{:S(2)}, u32[]{:S(2)}) collective-permute-start(bf16[1,10,8,128]{3,2,1,0:T(8,128)(2,1)S(1)} %get-tuple-element.99), channel_id=1, source_target_pairs={{0,28},{4,0},{8,4},{12,8},{16,12},{20,16},{24,20},{28,24},{1,29},{... | collective-permute-start | bytes 61448 | tf_op jit(solution)/shard_map/ppermute | solution.py:530
  124.8 19.0 %all-to-all-start.1 = ((bf16[32,64,128]{2,1,0:T(8,128)(2,1)}), bf16[32,64,128]{2,1,0:T(8,128)(2,1)S(1)}, u32[]{:S(2)}, u32[]{:S(2)}) async-start(bf16[32,64,128]{2,1,0:T(8,128)(2,1)} %broadcast_in_dim.14), calls=%async_computation.1 | async-start | bytes 1048576 | tf_op jit(solution)/shard_map/all_to_all | solution.py:560
  128.1 12.7 %collective-permute-start.18 = (bf16[8,1,8,128]{3,2,1,0:T(8,128)(2,1)S(1)}, bf16[8,1,8,128]{3,2,1,0:T(8,128)(2,1)S(1)}, u32[]{:S(2)}, u32[]{:S(2)}) collective-permute-start(bf16[8,1,8,128]{3,2,1,0:T(8,128)(2,1)S(1)} %get-tuple-element.102), channel_id=1, source_target_pairs={{0,1},{1,2},{2,3},{3,0},{4,5},{5,6},{6,7},{7,4},{8,9},{9,10},{10,1... | collective-permute-start | bytes 49160 | tf_op jit(solution)/shard_map/ppermute | solution.py:530
  129.5 11.3 %collective-permute-start.19 = (bf16[8,1,8,128]{3,2,1,0:T(8,128)(2,1)S(1)}, bf16[8,1,8,128]{3,2,1,0:T(8,128)(2,1)S(1)}, u32[]{:S(2)}, u32[]{:S(2)}) collective-permute-start(bf16[8,1,8,128]{3,2,1,0:T(8,128)(2,1)S(1)} %get-tuple-element.103), channel_id=1, source_target_pairs={{0,3},{1,0},{2,1},{3,2},{4,7},{5,4},{6,5},{7,6},{8,11},{9,8},{10,9... | collective-permute-start | bytes 49160 | tf_op jit(solution)/shard_map/ppermute | solution.py:530
